TPU v7x, 512 devices: a whole 4x8x8 slice. The times are simulated.
512 devices in a mesh: tile: 32 (over y, x), ir: 16 (over z, core).
Axes of the slice: x: 4, y: 8, z: 8, core: 2. Of those that a mesh axis runs over, the one named last changes fastest.
Arguments:
- samples: bfloat16 [4096, 1024], P(('tile', 'ir')), may hold values from -6 to 6
- ir_spectra: bfloat16 [16, 128, 2, 1024], P(None, 'ir'), may hold values from -0.5 to 0.5
- clip_lengths: int32 [16], replicated, may hold values from 1 to 1024, 4096 in all
- room_ids: int32 [16], replicated, may hold values from 0 to 15
Outputs:
- filtered: float32 [4096, 1024], P(('tile', 'ir'))
Inputs may be any that keep to these rules, and one draw needn't show every extreme that they name: `clip_lengths`: the lengths sum to 4096; clips lie end to end in block order.
All inputs are finite; a program needn't handle non-finite values.
Results may differ from a plain program's by a relative error of at most 0.0037.
Values may be sent and summed in bfloat16 or wider, within the bound.
A program may use at most 128 MiB of HBM per device.

v0:
```python
import jax
import jax.numpy as jnp
import numpy as np
from jax import lax
from jax.sharding import PartitionSpec as P


def from_behind(x, axis, by):
    length = lax.axis_size(axis)
    pairs = [(i, i + by) for i in range(length) if 0 <= i + by < length]
    return lax.ppermute(x, axis, pairs)


def in_blocks(x, dim, length):
    before, after = (x.shape[:dim], x.shape[dim + 1 :])
    return jnp.moveaxis(x.reshape(*before, length, -1, *after), dim, 0)


def sent_and_summed(x, axis, dim):
    tiles = in_blocks(x, dim, lax.axis_size(axis))
    arrived = lax.all_to_all(tiles, axis, split_axis=0, concat_axis=0, tiled=True)
    return arrived.sum(axis=0)


def forward_table(width):
    length = 2 * width
    sample = np.arange(length)
    bins = np.arange(width)
    phase = sample[:, None] * bins[None, :] % length
    angle = phase * (2.0 * np.pi / length)
    parity = np.where(sample % 2 == 0, 1.0, -1.0)
    sines = np.where(bins[None, :] == 0, parity[:, None], -np.sin(angle))
    table = np.concatenate([np.cos(angle), sines], axis=1)
    return jnp.asarray(table, dtype=jnp.float32).astype(jnp.bfloat16)


def inverse_table(width):
    length = 2 * width
    bins = np.arange(width)
    outputs = width + np.arange(width)
    phase = bins[:, None] * outputs[None, :] % length
    angle = phase * (2.0 * np.pi / length)
    weight = np.where(bins == 0, 1.0, 2.0)[:, None] / length
    parity = np.where(outputs % 2 == 0, 1.0, -1.0)[None, :] / length
    cosines = weight * np.cos(angle)
    sines = np.where(bins[:, None] == 0, parity, -weight * np.sin(angle))
    table = np.concatenate([cosines, sines], axis=0)
    return jnp.asarray(table, dtype=jnp.float32)


def packed_product(spectrum, response, width):
    are, aim = (spectrum[:, :width], spectrum[:, width:])
    hre, him = (response[:, :width], response[:, width:])
    cross = (jnp.arange(width, dtype=jnp.int32) > 0).astype(jnp.float32)[None, :]
    real = are * hre - cross * aim * him
    imag = cross * (are * him + aim * hre) + (1.0 - cross) * aim * him
    return jnp.concatenate([real, imag], axis=1)


def clip_info(clip_lengths, room_ids, blocks):
    ends = jnp.cumsum(clip_lengths)
    starts = ends - clip_lengths
    member = (blocks[:, None] >= starts[None, :]) & (blocks[:, None] < ends[None, :])
    begin = jnp.sum(jnp.where(member, starts[None, :], 0), axis=1)
    room = jnp.sum(jnp.where(member, room_ids[None, :], 0), axis=1)
    return (begin, room)


def on_device(samples, ir_spectra, clip_lengths, room_ids):
    rows, width = samples.shape
    groups = lax.axis_size("ir")
    count = rows * groups
    rooms, part_dev = (ir_spectra.shape[0], ir_spectra.shape[1])
    parts = part_dev * groups
    tile_base = lax.axis_index("tile") * count
    own_blocks = tile_base + lax.axis_index("ir") * rows + jnp.arange(rows, dtype=jnp.int32)
    own_begin, own_room = clip_info(clip_lengths, room_ids, own_blocks)
    before = from_behind(samples[rows - 1 :], ("tile", "ir"), 1)
    earlier = jnp.concatenate([before, samples[:-1]], axis=0)
    earlier = jnp.where((own_blocks == own_begin)[:, None], jnp.zeros_like(earlier), earlier)
    frames = jnp.concatenate([earlier, samples], axis=1)
    own_spectra = jnp.dot(frames, forward_table(width), preferred_element_type=jnp.float32).astype(
        jnp.bfloat16
    )
    blocks = tile_base + jnp.arange(count, dtype=jnp.int32)
    begin, room = clip_info(clip_lengths, room_ids, blocks)
    room_hot = (room[:, None] == jnp.arange(rooms, dtype=jnp.int32)[None, :]).astype(jnp.bfloat16)
    inverse = inverse_table(width)
    spectra = lax.all_gather(own_spectra, "ir", axis=0, tiled=True)
    delayed = from_behind(spectra[count - (parts - 1) :], "tile", 1)
    padded = jnp.concatenate([delayed, spectra], axis=0)
    flat_filters = ir_spectra.reshape(rooms, part_dev * 2 * width)
    selected = jnp.dot(room_hot, flat_filters, preferred_element_type=jnp.float32).astype(
        jnp.bfloat16
    )
    selected = selected.reshape(count, part_dev, 2 * width)
    first = lax.axis_index("ir") * part_dev

    def add_partition(index, summed):
        delay = first + index
        moved = lax.dynamic_slice_in_dim(padded, parts - 1 - delay, count, 0)
        chosen = lax.dynamic_index_in_dim(selected, index, 1, keepdims=False)
        live = blocks - delay >= begin
        term = packed_product(moved.astype(jnp.float32), chosen.astype(jnp.float32), width)
        return summed + jnp.where(live[:, None], term, jnp.zeros_like(term))

    summed = lax.fori_loop(0, part_dev, add_partition, jnp.zeros((count, 2 * width), jnp.float32))
    return sent_and_summed(
        jnp.dot(
            summed, inverse, precision=lax.Precision.HIGHEST, preferred_element_type=jnp.float32
        ),
        "ir",
        0,
    )


def solution(mesh):
    in_specs = (P(("tile", "ir"), None), P(None, "ir", None, None), P(), P())
    out_specs = P(("tile", "ir"), None)
    return jax.shard_map(
        on_device, mesh=mesh, in_specs=in_specs, out_specs=out_specs, check_vma=False
    )
```

profile of v0, /device:TPU:57, one launch (start us, length us, event | category | flops | bytes accessed | tf_op | source)
XLA Modules:
  0.0 96.7 jit_solution(4870245839410674996)
XLA Ops:
  0.0 0.8 slice.49
  0.8 4.5 %collective-permute-start = (bf16[1,1024]{1,0:T(2,128)(2,1)S(1)}, bf16[1,1024]{1,0:T(2,128)(2,1)S(1)}, u32[]{:S(2)}, u32[]{:S(2)}) collective-permute-start(bf16[1,1024]{1,0:T(2,128)(2,1)S(1)} %slice.49), channel_id=1, source_target_pairs={{0,1},{1,2},{2,3},{3,4},{4,5},{5,6},{6,7},{7,8},{8,9},{9,10},{10,1... | collective-permute-start | bytes 6152 | tf_op jit(solution)/shard_map/ppermute | solution.py:11
  5.4 0.7 copy.11
  6.3 0.7 sub.58
  6.9 2.8 %convolution_bitcast_fusion = f32[8,2048]{1,0:T(8,128)S(1)} fusion(bf16[1024,2048]{1,0:T(8,128)(2,1)} %constant.107, bf16[8,1024]{1,0:T(8,128)(2,1)} %param.8), kind=kOutput, calls=%fused_computation.14 | convolution fusion | flops 33554432 | bytes 4276224 | tf_op jit(solution)/shard_map/dot_general | solution.py:82
  10.0 0.4 reshape.73
  10.4 2.9 %fusion.5 = bf16[8,2048]{1,0:T(8,128)(2,1)S(1)} fusion(f32[8,2048]{1,0:T(8,128)S(1)} %convolution_bitcast_fusion, bf16[1024,2048]{1,0:T(8,128)(2,1)} %constant.106, bf16[7,1024]{1,0:T(8,128)(2,1)S(1)} %bitcast.23, bf16[1,1024]{1,0:T(2,128)(2,1)S(1)} %collective-permute-done, pred[8]{0:T(512)(128)(4,1)S(1)} %fusion.13), kind=kOutput, calls=%fused_computation.16 | convolution fusion | flops 33628160 | bytes 4309000 | tf_op jit(solution)/shard_map/dot_general | solution.py:82
  13.3 22.5 %all_gather.3 = bf16[128,2048]{1,0:T(8,128)(2,1)S(1)} all-gather(bf16[8,2048]{1,0:T(8,128)(2,1)S(1)} %fusion.5), channel_id=1, replica_groups=mesh['tile'=32,'ir'=16] {'ir'}, dimensions={0}, use_global_device_ids=true | all-gather | bytes 557056 | tf_op jit(solution)/shard_map/all_gather | solution.py:89
  35.9 3.1 %collective-permute-start.1 = (bf16[127,2048]{1,0:T(8,128)(2,1)S(1)}, bf16[127,2048]{1,0:T(8,128)(2,1)S(1)}, u32[]{:S(2)}, u32[]{:S(2)}) collective-permute-start(bf16[127,2048]{1,0:T(8,128)(2,1)S(1)} %slice.62), channel_id=1, source_target_pairs={{0,16},{16,32},{32,48},{48,64},{64,80},{80,96},{96,112},{112,128},... | collective-permute-start | bytes 1560584 | tf_op jit(solution)/shard_map/ppermute | solution.py:11
  39.1 1.3 %convolution_convert_fusion = bf16[128,16384]{1,0:T(8,128)(2,1)S(1)} fusion(bf16[16,16384]{1,0:T(8,128)(2,1)S(1)} %reshape.73, s32[128]{0:T(128)S(1)} %get-tuple-element.230), kind=kOutput, calls=%fused_computation.12 | convolution fusion | flops 69208064 | bytes 4719104 | tf_op jit(solution)/shard_map/dot_general | solution.py:93
  40.4 2.2 %copy.15 = bf16[16,8,8,2048]{3,2,0,1:T(8,128)(2,1)} copy(bf16[16,8,8,2048]{3,2,1,0:T(8,128)(2,1)S(1)} %bitcast.21) | data formatting | bytes 8388608 | tf_op jit(solution)/shard_map/reshape | solution.py:96
  42.6 10.5 %collective-permute-done.1 = bf16[127,2048]{1,0:T(8,128)(2,1)S(1)} collective-permute-done((bf16[127,2048]{1,0:T(8,128)(2,1)S(1)}, bf16[127,2048]{1,0:T(8,128)(2,1)S(1)}, u32[]{:S(2)}, u32[]{:S(2)}) %collective-permute-start.1) | collective-permute-done | bytes 520224 | tf_op jit(solution)/shard_map/ppermute | solution.py:11
  53.3 14.4 %while.16 = (s32[]{:T(128)}, f32[128,2048]{1,0:T(8,128)S(1)}, s32[]{:T(128)}, s32[128]{0:T(128)S(1)}, bf16[255,2048]{1,0:T(8,128)(2,1)S(1)}, /*index=5*/bf16[128...) while((s32[]{:T(128)}, f32[128,2048]{1,0:T(8,128)S(1)}, ...), condition=%wide.region_5.6_spmd.clone, body=%wide.region_4.5_spmd.clone.sunk | while | flops 3020168 | bytes 9454529 | solution.py:107
  53.5 1.1 %bitcast_convert_fusion.2 = f32[128,2048]{1,0:T(8,128)S(1)} fusion(bf16[128,8,2048]{2,0,1:T(8,128)(2,1)} %get-tuple-element.322, s32[]{:T(128)} %get-tuple-element.306), kind=kLoop, calls=%fused_computation.3.clone.1 | loop fusion | flops 262144 | bytes 1572868 | tf_op jit(solution)/shard_map/while/body/eval_jaxpr/convert_element_type | solution.py:104
  55.3 1.1 %bitcast_convert_fusion.2 = f32[128,2048]{1,0:T(8,128)S(1)} fusion(bf16[128,8,2048]{2,0,1:T(8,128)(2,1)} %get-tuple-element.322, s32[]{:T(128)} %get-tuple-element.306), kind=kLoop, calls=%fused_computation.3.clone.1 | loop fusion | flops 262144 | bytes 1572868 | tf_op jit(solution)/shard_map/while/body/eval_jaxpr/convert_element_type | solution.py:104
  57.1 1.1 %bitcast_convert_fusion.2 = f32[128,2048]{1,0:T(8,128)S(1)} fusion(bf16[128,8,2048]{2,0,1:T(8,128)(2,1)} %get-tuple-element.322, s32[]{:T(128)} %get-tuple-element.306), kind=kLoop, calls=%fused_computation.3.clone.1 | loop fusion | flops 262144 | bytes 1572868 | tf_op jit(solution)/shard_map/while/body/eval_jaxpr/convert_element_type | solution.py:104
  58.9 1.1 %bitcast_convert_fusion.2 = f32[128,2048]{1,0:T(8,128)S(1)} fusion(bf16[128,8,2048]{2,0,1:T(8,128)(2,1)} %get-tuple-element.322, s32[]{:T(128)} %get-tuple-element.306), kind=kLoop, calls=%fused_computation.3.clone.1 | loop fusion | flops 262144 | bytes 1572868 | tf_op jit(solution)/shard_map/while/body/eval_jaxpr/convert_element_type | solution.py:104
  60.7 1.1 %bitcast_convert_fusion.2 = f32[128,2048]{1,0:T(8,128)S(1)} fusion(bf16[128,8,2048]{2,0,1:T(8,128)(2,1)} %get-tuple-element.322, s32[]{:T(128)} %get-tuple-element.306), kind=kLoop, calls=%fused_computation.3.clone.1 | loop fusion | flops 262144 | bytes 1572868 | tf_op jit(solution)/shard_map/while/body/eval_jaxpr/convert_element_type | solution.py:104
  62.5 1.1 %bitcast_convert_fusion.2 = f32[128,2048]{1,0:T(8,128)S(1)} fusion(bf16[128,8,2048]{2,0,1:T(8,128)(2,1)} %get-tuple-element.322, s32[]{:T(128)} %get-tuple-element.306), kind=kLoop, calls=%fused_computation.3.clone.1 | loop fusion | flops 262144 | bytes 1572868 | tf_op jit(solution)/shard_map/while/body/eval_jaxpr/convert_element_type | solution.py:104
  64.3 1.1 %bitcast_convert_fusion.2 = f32[128,2048]{1,0:T(8,128)S(1)} fusion(bf16[128,8,2048]{2,0,1:T(8,128)(2,1)} %get-tuple-element.322, s32[]{:T(128)} %get-tuple-element.306), kind=kLoop, calls=%fused_computation.3.clone.1 | loop fusion | flops 262144 | bytes 1572868 | tf_op jit(solution)/shard_map/while/body/eval_jaxpr/convert_element_type | solution.py:104
  66.1 1.1 %bitcast_convert_fusion.2 = f32[128,2048]{1,0:T(8,128)S(1)} fusion(bf16[128,8,2048]{2,0,1:T(8,128)(2,1)} %get-tuple-element.322, s32[]{:T(128)} %get-tuple-element.306), kind=kLoop, calls=%fused_computation.3.clone.1 | loop fusion | flops 262144 | bytes 1572868 | tf_op jit(solution)/shard_map/while/body/eval_jaxpr/convert_element_type | solution.py:104
  67.7 7.2 %convolution_bitcast_fusion.1 = f32[16,8,1024]{2,1,0:T(8,128)S(1)} fusion(f32[128,2048]{1,0:T(8,128)S(1)} %get-tuple-element.181, f32[2048,1024]{1,0:T(8,128)} %constant.102.clone), kind=kOutput, calls=%fused_computation.17 | convolution fusion | flops 3221225472 | bytes 9961472 | tf_op jit(solution)/shard_map/dot_general | solution.py:109
  75.0 21.1 %all_to_all.5 = f32[16,8,1024]{2,1,0:T(8,128)S(1)} all-to-all(f32[16,8,1024]{2,1,0:T(8,128)S(1)} %convolution_bitcast_fusion.1), channel_id=1, replica_groups=mesh['tile'=32,'ir'=16] {'ir'}, dimensions={0} | all-to-all | bytes 1048576 | tf_op jit(solution)/shard_map/all_to_all | solution.py:21
  96.1 0.6 reduce_sum.39
  (65 shorter events, 5.4 us)
Async XLA Ops:
  0.0 10.4 %copy-start.1 = (bf16[8,1024]{1,0:T(8,128)(2,1)S(1)}, bf16[8,1024]{1,0:T(8,128)(2,1)}, u32[]{:S(2)}) copy-start(bf16[8,1024]{1,0:T(8,128)(2,1)} %param.8) | copy-start | bytes 49156
  0.0 10.0 %copy-start = (bf16[16,8,2,1024]{3,2,1,0:T(2,128)(2,1)S(1)}, bf16[16,8,2,1024]{3,2,1,0:T(2,128)(2,1)}, u32[]{:S(2)}) copy-start(bf16[16,8,2,1024]{3,2,1,0:T(2,128)(2,1)} %param.9) | copy-start | bytes 1572868
  0.8 9.6 %collective-permute-start = (bf16[1,1024]{1,0:T(2,128)(2,1)S(1)}, bf16[1,1024]{1,0:T(2,128)(2,1)S(1)}, u32[]{:S(2)}, u32[]{:S(2)}) collective-permute-start(bf16[1,1024]{1,0:T(2,128)(2,1)S(1)} %slice.49), channel_id=1, source_target_pairs={{0,1},{1,2},{2,3},{3,4},{4,5},{5,6},{6,7},{7,8},{8,9},{9,10},{10,1... | collective-permute-start | bytes 6152 | tf_op jit(solution)/shard_map/ppermute | solution.py:11
  9.8 29.2 %copy-start.2 = (s32[16]{0:T(128)S(1)}, s32[16]{0:T(128)}, u32[]{:S(2)}) copy-start(s32[16]{0:T(128)} %param.11) | copy-start | bytes 196
  35.9 17.3 %collective-permute-start.1 = (bf16[127,2048]{1,0:T(8,128)(2,1)S(1)}, bf16[127,2048]{1,0:T(8,128)(2,1)S(1)}, u32[]{:S(2)}, u32[]{:S(2)}) collective-permute-start(bf16[127,2048]{1,0:T(8,128)(2,1)S(1)} %slice.62), channel_id=1, source_target_pairs={{0,16},{16,32},{32,48},{48,64},{64,80},{80,96},{96,112},{112,128},... | collective-permute-start | bytes 1560584 | tf_op jit(solution)/shard_map/ppermute | solution.py:11
where the time goes:
time: 98.5 us; the launch traced here: 96.7 us
  blocking collectives  43.6 us (44%)
  other arithmetic  15.7 us (16%)
  matrix products  14.2 us (14%)
  waiting for transfers between devices  10.5 us (11%)
  starting transfers between devices  7.67 us (8%)
  local copies, waits for them, and re-layouts  4.3 us (4%)
    all_gather x1, blocking collectives, on_device(): spectra = lax.all_gather(own_spectra, 'ir', axis=0, tiled=True)  22.5 us
    all_to_all x1, blocking collectives, sent_and_summed(): lax.all_to_all(tiles, axis, split_axis=0, concat_axis=0, tiled=True)  21.1 us
    ppermute x2, waiting for transfers between devices, from_behind(): return lax.ppermute(x, axis, pairs)  10.5 us
    convert_element_type x8, other arithmetic, add_partition(): chosen.astype(jnp.float32)  9.15 us
    ppermute x2, starting transfers between devices, from_behind(): return lax.ppermute(x, axis, pairs)  7.67 us
    dot_general x1, matrix products, on_device(): jnp.dot(summed, inverse, precision=lax.Precision.HIGHEST, preferred_eleme...  7.22 us
    dot_general x2, matrix products, on_device(): jnp.dot(frames, forward_table(width), preferred_element_type=jnp.float32)  5.72 us
    reshape x1, local copies, waits for them, and re-layouts, on_device(): selected = selected.reshape(count, part_dev, 2 * width)  2.24 us
  transfers between devices with their start and end apart: 2, of which 1 were waited for; matrix products, arithmetic and copies ran while one was open for 9% of the time, Pallas kernels for 0%

commit v1 on v0

v1 whole, which is shorter than its diff:
```python
import jax
import jax.numpy as jnp
import numpy as np
from jax import lax
from jax.experimental import pallas as pl
from jax.experimental.pallas import tpu as pltpu
from jax.sharding import PartitionSpec as P

MESH = pl.DeviceIdType.MESH
W = 1024
ROWS = 8
CHIPS = 8
ROOMS = 16
PARTS = 16
OUT = 64
PAIRS = 5
SPAN = PAIRS * 2 * ROWS
SUB = 2 * W // 128
NONE = ROOMS * PARTS


def forward_half(width):
    length = 2 * width
    sample = np.arange(width)
    bins = np.arange(width)
    phase = sample[:, None] * bins[None, :] % length
    angle = phase * (2.0 * np.pi / length)
    parity = np.where(sample % 2 == 0, 1.0, -1.0)
    sines = np.where(bins[None, :] == 0, parity[:, None], -np.sin(angle))
    table = np.concatenate([np.cos(angle), sines], axis=1)
    return jnp.asarray(table, dtype=jnp.float32).astype(jnp.bfloat16)


def inverse_table(width):
    length = 2 * width
    bins = np.arange(width)
    outputs = width + np.arange(width)
    phase = bins[:, None] * outputs[None, :] % length
    angle = phase * (2.0 * np.pi / length)
    weight = np.where(bins == 0, 1.0, 2.0)[:, None] / length
    parity = np.where(outputs % 2 == 0, 1.0, -1.0)[None, :] / length
    cosines = weight * np.cos(angle)
    sines = np.where(bins[:, None] == 0, parity, -weight * np.sin(angle))
    table = np.concatenate([cosines, sines], axis=0)
    return jnp.asarray(table, dtype=jnp.float32).astype(jnp.bfloat16)


def kernel(
    samples,
    ir,
    lengths,
    rooms,
    forward,
    inverse,
    out,
    fwd_v,
    inv_v,
    ir_v,
    filters,
    unpacked,
    held,
    raw,
    spectra,
    summed,
    parts_out,
    arrived,
    choice_v,
    first_v,
    choice,
    first,
    lengths_s,
    rooms_s,
    small_sem,
    table_sem,
    ir_send,
    ir_recv,
    ir_own,
    in_send,
    in_recv,
    out_send,
    out_recv,
):
    tile, ir_at = lax.axis_index("tile"), lax.axis_index("ir")
    tiles = lax.axis_size("tile")
    z, c = ir_at // 2, ir_at % 2
    half = z // 4
    other = 2 * z + 1 - c

    get_lengths = pltpu.make_async_copy(lengths, lengths_s, small_sem.at[0])
    get_rooms = pltpu.make_async_copy(rooms, rooms_s, small_sem.at[1])
    get_lengths.start()
    get_rooms.start()

    barrier = pltpu.get_barrier_semaphore()

    def greet(to):
        pl.semaphore_signal(barrier, inc=1, device_id=to, device_id_type=MESH)

    def source(e, k):
        at = 8 + 4 * c - z - 1 + e
        return (tile + tiles - 1 + at // 8) % tiles, 2 * (at % 8) + k

    own_in = 2 * z + 1 - 4 * c
    for e in range(PAIRS):
        for k in range(2):

            @pl.when(jnp.logical_not((own_in == e) & (c == k)))
            def _(e=e, k=k):
                greet(source(e, k))

    for zs in range(CHIPS):

        @pl.when(jnp.logical_not((z == zs) & (half == c)))
        def _(zs=zs):
            greet((tile, 2 * zs + half))

    greet((tile, other))

    get_own = pltpu.make_async_copy(ir, ir_v.at[c], ir_own)
    get_own.start()
    get_forward = pltpu.make_async_copy(forward, fwd_v, table_sem.at[0])
    get_forward.start()
    get_inverse = pltpu.make_async_copy(inverse, inv_v, table_sem.at[1])
    get_inverse.start()

    own_is_in = ((own_in >= 0) & (own_in < PAIRS)).astype(jnp.int32)
    own_is_out = (half == c).astype(jnp.int32)
    pl.semaphore_wait(barrier, 2 * PAIRS + CHIPS + 1 - own_is_in - own_is_out)

    def target(e, d):
        at = 8 + 4 * d - 1 + e - z
        return (tile + 1 - at // 8) % tiles, 2 * (at % 8) + d

    for e in range(PAIRS):
        for d in range(2):
            itself = (own_in == e) & (c == d)

            @pl.when(itself)
            def _(e=e, d=d):
                pltpu.make_async_copy(samples, held.at[e, c], in_recv.at[e, c]).start()

            @pl.when(jnp.logical_not(itself))
            def _(e=e, d=d):
                pltpu.make_async_remote_copy(
                    src_ref=samples,
                    dst_ref=held.at[e, c],
                    send_sem=in_send.at[e, d],
                    recv_sem=in_recv.at[e, c],
                    device_id=target(e, d),
                    device_id_type=MESH,
                ).start()

    send_ir = pltpu.make_async_remote_copy(
        src_ref=ir,
        dst_ref=ir_v.at[c],
        send_sem=ir_send,
        recv_sem=ir_recv,
        device_id=(tile, other),
        device_id_type=MESH,
    )
    send_ir.start()

    get_lengths.wait()
    get_rooms.wait()
    place = lax.broadcasted_iota(jnp.int32, (8, 128), 0) * 128 + lax.broadcasted_iota(
        jnp.int32, (8, 128), 1
    )
    block = tile * (2 * OUT) + c * OUT + place // PARTS
    delay = z * PARTS + place % PARTS
    row_block = tile * (2 * OUT) + c * OUT - z * PARTS - PARTS + place
    begin = jnp.zeros((8, 128), jnp.int32)
    room = jnp.zeros((8, 128), jnp.int32)
    joined = jnp.ones((8, 128), jnp.float32)
    start = jnp.int32(0)
    for n in range(ROOMS):
        end = start + lengths_s[n]
        member = (block >= start) & (block < end)
        begin = jnp.where(member, start, begin)
        room = jnp.where(member, rooms_s[n], room)
        joined = jnp.where(row_block == start, 0.0, joined)
        start = end
    chosen = jnp.where(block - delay >= begin, room * PARTS + place % PARTS, NONE)
    choice_v[...] = chosen
    first_v[...] = joined
    put_choice = pltpu.make_async_copy(choice_v, choice, small_sem.at[2])
    put_first = pltpu.make_async_copy(first_v, first, small_sem.at[3])
    put_choice.start()
    put_first.start()

    corner = (lax.broadcasted_iota(jnp.int32, (8, 128), 0) == 0) & (
        lax.broadcasted_iota(jnp.int32, (8, 128), 1) == 0
    )
    filters[NONE] = jnp.zeros((3, 8, 128), jnp.float32)

    def unpack(part):
        def step(n, _):
            for p in range(8):
                unpacked[pl.ds(16 * p, 16), :] = ir_v[part, n, p].astype(jnp.float32)
            for p in range(8):
                hre = unpacked[pl.ds(16 * p, 8, stride=2), :]
                him = unpacked[pl.ds(16 * p + 1, 8, stride=2), :]
                at = n * PARTS + part * 8 + p
                filters[at, 0] = hre
                filters[at, 1] = jnp.where(corner, 0.0, him)
                filters[at, 2] = jnp.where(corner, him, hre)
            return 0

        lax.fori_loop(0, ROOMS, step, 0)

    get_own.wait()
    unpack(c)
    send_ir.wait_recv()
    unpack(1 - c)

    put_choice.wait()
    put_first.wait()
    get_forward.wait()
    for e in range(PAIRS):
        for k in range(2):
            pltpu.make_async_copy(samples, held.at[e, k], in_recv.at[e, k]).wait()

    x = held[...].astype(jnp.float32).reshape(SPAN, W).astype(jnp.bfloat16)
    for n in range(2 * W // 256):
        g = jnp.dot(x, fwd_v[:, 256 * n : 256 * n + 256], preferred_element_type=jnp.float32)
        raw[pl.ds(2 * n, SPAN, stride=SUB), :] = g[:, :128]
        raw[pl.ds(2 * n + 1, SPAN, stride=SUB), :] = g[:, 128:]

    sign = 1.0 - 2.0 * (lax.broadcasted_iota(jnp.int32, (SUB, 128), 1) % 2).astype(jnp.float32)
    for r in range(1, SPAN):
        before = raw[pl.ds(SUB * (r - 1), SUB), :]
        own = raw[pl.ds(SUB * r, SUB), :]
        both = first[r // 128, r % 128] * before + sign * own
        spectra[pl.ds(SUB * r, SUB), :] = both.astype(jnp.bfloat16).astype(jnp.float32)

    def eight(b, _):
        res = [jnp.zeros((8, 128), jnp.float32) for _ in range(8)]
        ims = [jnp.zeros((8, 128), jnp.float32) for _ in range(8)]
        for p in range(PARTS):
            for t in range(8):
                at = pl.multiple_of(SUB * (8 * b + t - p + PARTS), 8)
                are = spectra[pl.ds(at, 8), :]
                aim = spectra[pl.ds(at + 8, 8), :]
                h = choice[b, 16 * t + p]
                h0, h1, h2 = filters[h, 0], filters[h, 1], filters[h, 2]
                res[t] = res[t] + (are * h0 - aim * h1)
                ims[t] = ims[t] + (are * h1 + aim * h2)
        for t in range(8):
            to = pl.multiple_of(SUB * (8 * b + t), 8)
            summed[pl.ds(to, 8), :] = res[t]
            summed[pl.ds(to + 8, 8), :] = ims[t]
        return 0

    lax.fori_loop(0, OUT // 8, eight, 0)

    get_inverse.wait()
    y = jnp.concatenate(
        [summed[pl.ds(j, OUT, stride=SUB), :].astype(jnp.bfloat16) for j in range(SUB)], axis=1
    )
    for n in range(W // 256):
        v = jnp.dot(y, inv_v[:, 256 * n : 256 * n + 256], preferred_element_type=jnp.float32)
        for g in range(8):
            parts_out[g, :, 256 * n : 256 * n + 256] = v[8 * g : 8 * g + 8].astype(jnp.bfloat16)

    for g in range(4):
        for k in range(2):
            itself = (z == 4 * c + g) & (c == k)

            @pl.when(itself)
            def _(g=g, k=k):
                pltpu.make_async_copy(
                    parts_out.at[2 * g + k], arrived.at[z], out_recv.at[z]
                ).start()

            @pl.when(jnp.logical_not(itself))
            def _(g=g, k=k):
                pltpu.make_async_remote_copy(
                    src_ref=parts_out.at[2 * g + k],
                    dst_ref=arrived.at[z],
                    send_sem=out_send.at[2 * g + k],
                    recv_sem=out_recv.at[z],
                    device_id=(tile, 2 * (4 * c + g) + k),
                    device_id_type=MESH,
                ).start()

    total = jnp.zeros((ROWS, W), jnp.float32)
    for zs in range(CHIPS):
        pltpu.make_async_copy(parts_out.at[0], arrived.at[zs], out_recv.at[zs]).wait()
        total = total + arrived[zs].astype(jnp.float32)
    out[...] = total

    send_ir.wait_send()
    for e in range(PAIRS):
        for d in range(2):

            @pl.when(jnp.logical_not((own_in == e) & (c == d)))
            def _(e=e, d=d):
                pltpu.make_async_copy(samples, held.at[e, 0], in_send.at[e, d]).wait()

    for g in range(4):
        for k in range(2):

            @pl.when(jnp.logical_not((z == 4 * c + g) & (c == k)))
            def _(g=g, k=k):
                pltpu.make_async_copy(
                    parts_out.at[2 * g + k], arrived.at[0], out_send.at[2 * g + k]
                ).wait()


def on_device(samples, ir_spectra, clip_lengths, room_ids):
    rooms, parts = ir_spectra.shape[0], ir_spectra.shape[1]
    ir = ir_spectra.reshape(rooms, parts, 2, W // 128, 128)
    ir = ir.transpose(0, 1, 3, 2, 4).reshape(rooms, parts, SUB, 128)
    hbm = pl.BlockSpec(memory_space=pl.ANY)
    bf16, f32, dma = jnp.bfloat16, jnp.float32, pltpu.SemaphoreType.DMA
    return pl.pallas_call(
        kernel,
        out_shape=jax.ShapeDtypeStruct((ROWS, W), f32),
        in_specs=[hbm] * 6,
        out_specs=pl.BlockSpec(memory_space=pltpu.VMEM),
        scratch_shapes=[
            pltpu.VMEM((W, 2 * W), bf16),
            pltpu.VMEM((2 * W, W), bf16),
            pltpu.VMEM((2, ROOMS, 8, SUB, 128), bf16),
            pltpu.VMEM((NONE + 1, 3, 8, 128), f32),
            pltpu.VMEM((128, 128), f32),
            pltpu.VMEM((PAIRS, 2, ROWS, W), bf16),
            pltpu.VMEM((SPAN * SUB, 128), f32),
            pltpu.VMEM((SPAN * SUB, 128), f32),
            pltpu.VMEM((OUT * SUB, 128), f32),
            pltpu.VMEM((8, ROWS, W), bf16),
            pltpu.VMEM((CHIPS, ROWS, W), bf16),
            pltpu.VMEM((8, 128), jnp.int32),
            pltpu.VMEM((8, 128), f32),
            pltpu.SMEM((8, 128), jnp.int32),
            pltpu.SMEM((8, 128), f32),
            pltpu.SMEM((ROOMS,), jnp.int32),
            pltpu.SMEM((ROOMS,), jnp.int32),
            dma((4,)),
            dma((2,)),
            dma,
            dma,
            dma,
            dma((PAIRS, 2)),
            dma((PAIRS, 2)),
            dma((8,)),
            dma((CHIPS,)),
        ],
        compiler_params=pltpu.CompilerParams(
            collective_id=0, has_side_effects=True, vmem_limit_bytes=48 * 1024 * 1024
        ),
    )(samples, ir, clip_lengths, room_ids, forward_half(W), inverse_table(W))


def solution(mesh):
    in_specs = (P(("tile", "ir"), None), P(None, "ir", None, None), P(), P())
    out_specs = P(("tile", "ir"), None)
    return jax.shard_map(
        on_device, mesh=mesh, in_specs=in_specs, out_specs=out_specs, check_vma=False
    )
```

time: 98.5 us -> 36.5 us (0.37)
  the two profiles are of different devices: /device:TPU:57 before, /device:TPU:1 now
where the time goes in v1:
time: 36.5 us; the launch traced here: 36.2 us
  Pallas kernels  30.3 us (83%)
  local copies, waits for them, and re-layouts  5.87 us (16%)
    pallas_call x1, Pallas kernels, on_device(): pl.pallas_call(kernel, out_shape=jax.ShapeDtypeStruct((ROWS, W), f32), in...  30.3 us
    unnamed x11, local copies, waits for them, and re-layouts  5.87 us

profile of v1, /device:TPU:1, one launch (start us, length us, event | category | flops | bytes accessed | tf_op | source)
XLA Modules:
  0.0 36.2 jit_solution(18248449958859664194)
XLA Ops:
  0.0 0.0 copy-start
  0.0 2.2 %copy-done = bf16[1024,2048]{1,0:T(8,128)(2,1)S(1)} copy-done((bf16[1024,2048]{1,0:T(8,128)(2,1)S(1)}, bf16[1024,2048]{1,0:T(8,128)(2,1)}, u32[]{:S(2)}) %copy-start) | copy-done | bytes 4194328
  2.2 0.0 copy-start.1
  2.2 1.0 %copy-done.1 = bf16[16,8,2,1024]{3,2,1,0:T(2,128)(2,1)S(1)} copy-done((bf16[16,8,2,1024]{3,2,1,0:T(2,128)(2,1)S(1)}, bf16[16,8,2,1024]{3,2,1,0:T(2,128)(2,1)}, u32[]{:S(2)}) %copy-start.1) | copy-done | bytes 524312
  3.2 0.0 copy-start.2
  3.2 0.7 %copy-done.2 = bf16[8,1024]{1,0:T(8,128)(2,1)S(1)} copy-done((bf16[8,1024]{1,0:T(8,128)(2,1)S(1)}, bf16[8,1024]{1,0:T(8,128)(2,1)}, u32[]{:S(2)}) %copy-start.2) | copy-done | bytes 16408
  3.9 0.0 copy-start.3
  4.0 0.7 %copy-done.3 = s32[16]{0:T(128)S(1)} copy-done((s32[16]{0:T(128)S(1)}, s32[16]{0:T(128)}, u32[]{:S(2)}) %copy-start.3) | copy-done | bytes 88
  4.6 0.0 copy-start.4
  4.6 0.7 %copy-done.4 = s32[16]{0:T(128)S(1)} copy-done((s32[16]{0:T(128)S(1)}, s32[16]{0:T(128)}, u32[]{:S(2)}) %copy-start.4) | copy-done | bytes 88
  5.3 30.3 %shard_map.64 = f32[8,1024]{1,0:T(8,128)S(1)} custom-call(bf16[8,1024]{1,0:T(8,128)(2,1)S(1)} %copy-done.2, bf16[16,8,16,128]{3,2,1,0:T(8,128)(2,1)S(1)} %bitcast.5, s32[16]{0:T(128)S(1)} %copy-done.3, s32[16]{0:T(128)S(1)} %copy-done.4, bf16[1024,2048]{1,0:T(8,128)(2,1)S(1)} %copy-done, bf16[2048,1024]{1,0:T(8,128)(2,1)} %constant.9.inverse), custom_call_target="tpu_custom_call" | custom-call | tf_op jit(solution)/shard_map/pallas_call | solution.py:315
  35.6 0.6 %copy.9 = f32[8,1024]{1,0:T(8,128)} copy(f32[8,1024]{1,0:T(8,128)S(1)} %shard_map.64) | data formatting | bytes 65536
Async XLA Ops:
  0.0 2.2 %copy-start = (bf16[1024,2048]{1,0:T(8,128)(2,1)S(1)}, bf16[1024,2048]{1,0:T(8,128)(2,1)}, u32[]{:S(2)}) copy-start(bf16[1024,2048]{1,0:T(8,128)(2,1)} %constant.8.forward) | copy-start | bytes 12582916
  2.2 1.0 %copy-start.1 = (bf16[16,8,2,1024]{3,2,1,0:T(2,128)(2,1)S(1)}, bf16[16,8,2,1024]{3,2,1,0:T(2,128)(2,1)}, u32[]{:S(2)}) copy-start(bf16[16,8,2,1024]{3,2,1,0:T(2,128)(2,1)} %param.7) | copy-start | bytes 1572868
  3.2 0.7 %copy-start.2 = (bf16[8,1024]{1,0:T(8,128)(2,1)S(1)}, bf16[8,1024]{1,0:T(8,128)(2,1)}, u32[]{:S(2)}) copy-start(bf16[8,1024]{1,0:T(8,128)(2,1)} %samples.1) | copy-start | bytes 49156
  3.9 0.7 %copy-start.3 = (s32[16]{0:T(128)S(1)}, s32[16]{0:T(128)}, u32[]{:S(2)}) copy-start(s32[16]{0:T(128)} %lengths.1) | copy-start | bytes 196
  4.6 0.7 %copy-start.4 = (s32[16]{0:T(128)S(1)}, s32[16]{0:T(128)}, u32[]{:S(2)}) copy-start(s32[16]{0:T(128)} %rooms.1) | copy-start | bytes 196

commit v2 on v1

--- a/solution.py
+++ b/solution.py
@@ -310,7 +310,7 @@
     rooms, parts = ir_spectra.shape[0], ir_spectra.shape[1]
     ir = ir_spectra.reshape(rooms, parts, 2, W // 128, 128)
     ir = ir.transpose(0, 1, 3, 2, 4).reshape(rooms, parts, SUB, 128)
-    hbm = pl.BlockSpec(memory_space=pl.ANY)
+    hbm = pl.BlockSpec(memory_space=pltpu.HBM)
     bf16, f32, dma = jnp.bfloat16, jnp.float32, pltpu.SemaphoreType.DMA
     return pl.pallas_call(
         kernel,
@@ -346,7 +346,7 @@
             dma((CHIPS,)),
         ],
         compiler_params=pltpu.CompilerParams(
-            collective_id=0, has_side_effects=True, vmem_limit_bytes=48 * 1024 * 1024
+            collective_id=0, has_side_effects=True, vmem_limit_bytes=67_043_328
         ),
     )(samples, ir, clip_lengths, room_ids, forward_half(W), inverse_table(W))
 

time: 36.5 us -> 32.7 us (0.90)
  local copies, waits for them, and re-layouts: 5.87 us -> 1.38 us
  Pallas kernels: 30.3 us -> 31.1 us
    unnamed x11 -> x1, local copies, waits for them, and re-layouts: 5.87 us -> 1.38 us
    pallas_call x1, Pallas kernels: 30.3 us -> 31.1 us  [on_device(): pl.pallas_call(kernel, out_shape=jax.ShapeDtypeStruct((ROWS, W), f32), in...]
where the time goes in v2:
time: 32.7 us; the launch traced here: 32.5 us
  Pallas kernels  31.1 us (95%)
  local copies, waits for them, and re-layouts  1.38 us (4%)
    pallas_call x1, Pallas kernels, on_device(): pl.pallas_call(kernel, out_shape=jax.ShapeDtypeStruct((ROWS, W), f32), in...  31.1 us
    unnamed x1, local copies, waits for them, and re-layouts  1.38 us

profile of v2, /device:TPU:1, one launch (start us, length us, event | category | flops | bytes accessed | tf_op | source)
XLA Modules:
  0.0 32.5 jit_solution(1402435087284387230)
XLA Ops:
  0.0 31.1 %shard_map.64 = f32[8,1024]{1,0:T(8,128)} custom-call(bf16[8,1024]{1,0:T(8,128)(2,1)} %samples.1, bf16[16,8,16,128]{3,2,1,0:T(8,128)(2,1)} %bitcast.5, s32[16]{0:T(128)} %lengths.1, s32[16]{0:T(128)} %rooms.1, bf16[1024,2048]{1,0:T(8,128)(2,1)} %constant.8.forward, bf16[2048,1024]{1,0:T(8,128)(2,1)} %constant.9.inverse), custom_call_target="tpu_custom_call" | custom-call | tf_op jit(solution)/shard_map/pallas_call | solution.py:315
  31.1 1.4 %copy.9 = f32[8,1024]{1,0:T(8,128)} copy(f32[8,1024]{1,0:T(8,128)} %shard_map.64) | data formatting | bytes 65536

commit v3 on v2

v3 whole, which is shorter than its diff:
```python
import jax
import jax.numpy as jnp
import numpy as np
from jax import lax
from jax.experimental import pallas as pl
from jax.experimental.pallas import tpu as pltpu
from jax.sharding import PartitionSpec as P

MESH = pl.DeviceIdType.MESH
W = 1024
ROWS = 8
CHIPS = 8
ROOMS = 16
PARTS = 16
OUT = 64
PAIRS = 5
SPAN = PAIRS * 2 * ROWS
SUB = 2 * W // 128
NONE = ROOMS * PARTS


def forward_part(width):
    length = 2 * width
    sample = np.arange(width // 2)
    bins = np.arange(width)
    phase = sample[:, None] * bins[None, :] % length
    angle = phase * (2.0 * np.pi / length)
    parity = np.where(sample % 2 == 0, 1.0, -1.0)
    sines = np.where(bins[None, :] == 0, parity[:, None], -np.sin(angle))
    table = np.concatenate([np.cos(angle), sines], axis=1)
    return jnp.asarray(table, dtype=jnp.float32).astype(jnp.bfloat16)


def inverse_part(width):
    length = 2 * width
    bins = np.arange(width)
    outputs = width + np.arange(width // 2)
    phase = bins[:, None] * outputs[None, :] % length
    angle = phase * (2.0 * np.pi / length)
    weight = np.where(bins == 0, 1.0, 2.0)[:, None] / length
    parity = np.where(outputs % 2 == 0, 1.0, -1.0)[None, :] / length
    cosines = weight * np.cos(angle)
    sines = np.where(bins[:, None] == 0, parity, -weight * np.sin(angle))
    table = np.concatenate([cosines, sines], axis=0)
    return jnp.asarray(table, dtype=jnp.float32).astype(jnp.bfloat16)


def kernel(
    samples,
    ir,
    lengths,
    rooms,
    forward,
    inverse,
    out,
    fwd_v,
    inv_v,
    ir_v,
    filters,
    unpacked,
    held,
    raw,
    spectra,
    last,
    summed,
    parts_out,
    arrived,
    choice_v,
    first_v,
    choice,
    first,
    lengths_s,
    rooms_s,
    small_sem,
    table_sem,
    ir_send,
    ir_recv,
    ir_own,
    in_send,
    in_recv,
    out_send,
    out_recv,
):
    tile, ir_at = lax.axis_index("tile"), lax.axis_index("ir")
    tiles = lax.axis_size("tile")
    z, c = ir_at // 2, ir_at % 2
    half = z // 4
    other = 2 * z + 1 - c
    far_first = (4, 3, 5, 2, 6, 1, 7, 0)

    get_lengths = pltpu.make_async_copy(lengths, lengths_s, small_sem.at[0])
    get_rooms = pltpu.make_async_copy(rooms, rooms_s, small_sem.at[1])
    get_lengths.start()
    get_rooms.start()

    @pl.when(tile == 0)
    def _():
        held[...] = jnp.zeros(held.shape, held.dtype)

    barrier = pltpu.get_barrier_semaphore()

    def greet(to):
        pl.semaphore_signal(barrier, inc=1, device_id=to, device_id_type=MESH)

    for away in far_first:
        e = (2 * z + away + 9 - 4 * c) % 8
        before = (4 * c + e < z + 1).astype(jnp.int32)
        at = (z + away) % 8
        for k in range(2):
            real = (e < PAIRS) & ((before == 0) | (tile > 0))
            if away == 0:
                real = real & ((before == 1) | (c != k))

            @pl.when(real)
            def _(before=before, at=at, k=k):
                greet(((tile + tiles - before) % tiles, 2 * at + k))

        if away == 0:

            @pl.when(half != c)
            def _(at=at):
                greet((tile, 2 * at + half))

        else:
            greet((tile, 2 * at + half))
    greet((tile, other))

    get_own = pltpu.make_async_copy(ir, ir_v.at[c], ir_own)
    get_own.start()
    get_forward = pltpu.make_async_copy(forward, fwd_v, table_sem.at[0])
    get_forward.start()
    get_inverse = pltpu.make_async_copy(inverse, inv_v, table_sem.at[1])
    get_inverse.start()

    get_lengths.wait()
    get_rooms.wait()
    place = lax.broadcasted_iota(jnp.int32, (8, 128), 0) * 128 + lax.broadcasted_iota(
        jnp.int32, (8, 128), 1
    )
    block = tile * (2 * OUT) + c * OUT + place // PARTS
    delay = z * PARTS + place % PARTS
    row_block = tile * (2 * OUT) + c * OUT - z * PARTS - PARTS + place
    begin = jnp.zeros((8, 128), jnp.int32)
    room = jnp.zeros((8, 128), jnp.int32)
    joined = jnp.ones((8, 128), jnp.float32)
    start = jnp.int32(0)
    for n in range(ROOMS):
        end = start + lengths_s[n]
        member = (block >= start) & (block < end)
        begin = jnp.where(member, start, begin)
        room = jnp.where(member, rooms_s[n], room)
        joined = jnp.where(row_block == start, 0.0, joined)
        start = end
    chosen = jnp.where(block - delay >= begin, room * PARTS + place % PARTS, NONE)
    choice_v[...] = chosen
    first_v[...] = joined
    put_choice = pltpu.make_async_copy(choice_v, choice, small_sem.at[2])
    put_first = pltpu.make_async_copy(first_v, first, small_sem.at[3])
    put_choice.start()
    put_first.start()

    corner = (lax.broadcasted_iota(jnp.int32, (8, 128), 0) == 0) & (
        lax.broadcasted_iota(jnp.int32, (8, 128), 1) == 0
    )
    filters[NONE] = jnp.zeros((3, 8, 128), jnp.float32)

    def unpack(part):
        def step(n, _):
            for p in range(8):
                unpacked[pl.ds(16 * p, 16), :] = ir_v[part, n, p].astype(jnp.float32)
            for p in range(8):
                hre = unpacked[pl.ds(16 * p, 8, stride=2), :]
                him = unpacked[pl.ds(16 * p + 1, 8, stride=2), :]
                at = n * PARTS + part * 8 + p
                filters[at, 0] = hre
                filters[at, 1] = jnp.where(corner, 0.0, him)
                filters[at, 2] = jnp.where(corner, him, hre)
            return 0

        lax.fori_loop(0, ROOMS, step, 0)

    get_own.wait()
    unpack(c)
    last[...] = jnp.zeros(last.shape, jnp.float32)

    own_is_in = ((c == z // 2) & (z < 4)).astype(jnp.int32)
    own_is_out = (half == c).astype(jnp.int32)
    crossing = jnp.minimum(z + 1, PAIRS) + jnp.maximum(z - 3, 0)
    crossing = crossing * (tile == tiles - 1).astype(jnp.int32)
    pl.semaphore_wait(barrier, 2 * PAIRS + CHIPS + 1 - own_is_in - own_is_out - crossing)

    def send_samples(e, d):
        ahead = (4 * d + e < z + 1).astype(jnp.int32)

        @pl.when((ahead == 0) | (tile < tiles - 1))
        def _():
            pltpu.make_async_remote_copy(
                src_ref=samples,
                dst_ref=held.at[e, c],
                send_sem=in_send.at[e, d],
                recv_sem=in_recv.at[e, c],
                device_id=((tile + ahead) % tiles, 2 * ((4 * d + e + 7 - z) % 8) + d),
                device_id_type=MESH,
            ).start()

    for away in far_first:
        place_on_ring = (2 * z + away) % 8
        d, e = place_on_ring // 4, place_on_ring % 4 + 1
        if away == 0:
            itself = own_is_in == 1

            @pl.when(itself)
            def _(e=e):
                pltpu.make_async_copy(samples, held.at[e, c], in_recv.at[e, c]).start()

            @pl.when(jnp.logical_not(itself))
            def _(e=e, d=d):
                send_samples(e, d)

        else:
            send_samples(e, d)

        @pl.when(e == 4)
        def _(d=d):
            send_samples(0, 1 - d)

    send_ir = pltpu.make_async_remote_copy(
        src_ref=ir,
        dst_ref=ir_v.at[c],
        send_sem=ir_send,
        recv_sem=ir_recv,
        device_id=(tile, other),
        device_id_type=MESH,
    )
    send_ir.start()

    put_choice.wait()
    put_first.wait()
    get_forward.wait()
    get_inverse.wait()
    send_ir.wait_recv()
    unpack(1 - c)

    lane = lax.broadcasted_iota(jnp.int32, (8, 128), 1) % 4
    turn_re = jnp.where(lane == 0, 1.0, jnp.where(lane == 2, -1.0, 0.0))
    turn_im = jnp.where(lane == 1, 1.0, jnp.where(lane == 3, -1.0, 0.0))
    sign = 1.0 - 2.0 * (lane % 2).astype(jnp.float32)

    def pair(e, _):
        @pl.when((tile > 0) | (4 * c + e >= z + 1))
        def _():
            for k in range(2):
                pltpu.make_async_copy(samples, held.at[e, k], in_recv.at[e, k]).wait()

        x = held[e].astype(jnp.float32).reshape(16, W)
        x = jnp.concatenate([x[:, : W // 2], x[:, W // 2 :]], axis=0).astype(jnp.bfloat16)
        for n in range(2 * W // 256):
            g = jnp.dot(x, fwd_v[:, 256 * n : 256 * n + 256], preferred_element_type=jnp.float32)
            raw[pl.ds(2 * n, 32, stride=SUB), :] = g[:, :128]
            raw[pl.ds(2 * n + 1, 32, stride=SUB), :] = g[:, 128:]
        before_re, before_im = last[0], last[1]
        for r in range(16):
            first_re, first_im = raw[SUB * r : SUB * r + 8, :], raw[SUB * r + 8 : SUB * r + 16, :]
            at = SUB * (16 + r)
            then_re, then_im = raw[at : at + 8, :], raw[at + 8 : at + 16, :]
            own_re = first_re + (turn_re * then_re + turn_im * then_im)
            own_im = first_im + (turn_re * then_im - turn_im * then_re)
            opens = first[e // 8, 16 * e + r]
            frame_re = opens * before_re + sign * own_re
            frame_im = opens * before_im + sign * own_im
            to = pl.multiple_of(SUB * (16 * e + r), 8)
            spectra[pl.ds(to, 8), :] = frame_re.astype(jnp.bfloat16).astype(jnp.float32)
            spectra[pl.ds(to + 8, 8), :] = frame_im.astype(jnp.bfloat16).astype(jnp.float32)
            before_re, before_im = own_re, own_im
        last[0] = before_re
        last[1] = before_im

        @pl.when(e > 0)
        def _():
            g = e - 1

            def eight(b, _):
                res = [jnp.zeros((8, 128), jnp.float32) for _ in range(8)]
                ims = [jnp.zeros((8, 128), jnp.float32) for _ in range(8)]
                for p in range(PARTS):
                    for t in range(8):
                        at = pl.multiple_of(SUB * (16 * g + 8 * b + t - p + PARTS), 8)
                        are = spectra[pl.ds(at, 8), :]
                        aim = spectra[pl.ds(at + 8, 8), :]
                        h = choice[2 * g + b, 16 * t + p]
                        h0, h1, h2 = filters[h, 0], filters[h, 1], filters[h, 2]
                        res[t] = res[t] + (are * h0 - aim * h1)
                        ims[t] = ims[t] + (are * h1 + aim * h2)
                for t in range(8):
                    to = pl.multiple_of(SUB * (8 * b + t), 8)
                    summed[pl.ds(to, 8), :] = res[t]
                    summed[pl.ds(to + 8, 8), :] = ims[t]
                    summed[pl.ds(16 * SUB + to, 8), :] = turn_re * res[t] - turn_im * ims[t]
                    summed[pl.ds(16 * SUB + to + 8, 8), :] = turn_re * ims[t] + turn_im * res[t]
                return 0

            lax.fori_loop(0, 2, eight, 0)

            y = jnp.concatenate(
                [summed[pl.ds(j, 32, stride=SUB), :].astype(jnp.bfloat16) for j in range(SUB)],
                axis=1,
            )
            for n in range(W // 512):
                v = jnp.dot(
                    y, inv_v[:, 256 * n : 256 * n + 256], preferred_element_type=jnp.float32
                )
                for q in range(4):
                    left = 512 * (q // 2) + 256 * n
                    parts_out[2 * g + q % 2, :, left : left + 256] = v[8 * q : 8 * q + 8].astype(
                        jnp.bfloat16
                    )
            for k in range(2):
                itself = (z == 4 * c + g) & (c == k)

                @pl.when(itself)
                def _(k=k):
                    pltpu.make_async_copy(
                        parts_out.at[2 * g + k], arrived.at[z], out_recv.at[z]
                    ).start()

                @pl.when(jnp.logical_not(itself))
                def _(k=k):
                    pltpu.make_async_remote_copy(
                        src_ref=parts_out.at[2 * g + k],
                        dst_ref=arrived.at[z],
                        send_sem=out_send.at[2 * g + k],
                        recv_sem=out_recv.at[z],
                        device_id=(tile, 2 * (4 * c + g) + k),
                        device_id_type=MESH,
                    ).start()

        return 0

    lax.fori_loop(0, PAIRS, pair, 0)

    send_ir.wait_send()
    for e in range(PAIRS):
        for d in range(2):
            itself = (own_is_in == 1) & (4 * d + e == 2 * z + 1) & (c == d)
            crosses = (4 * d + e < z + 1) & (tile == tiles - 1)

            @pl.when(jnp.logical_not(itself | crosses))
            def _(e=e, d=d):
                pltpu.make_async_copy(samples, held.at[e, 0], in_send.at[e, d]).wait()

    for g in range(4):
        for k in range(2):

            @pl.when(jnp.logical_not((z == 4 * c + g) & (c == k)))
            def _(g=g, k=k):
                pltpu.make_async_copy(
                    parts_out.at[2 * g + k], arrived.at[0], out_send.at[2 * g + k]
                ).wait()

    total = jnp.zeros((ROWS, W), jnp.float32)
    for zs in range(CHIPS):
        pltpu.make_async_copy(parts_out.at[0], arrived.at[zs], out_recv.at[zs]).wait()
        total = total + arrived[zs].astype(jnp.float32)
    out[...] = total


def on_device(samples, ir_spectra, clip_lengths, room_ids):
    rooms, parts = ir_spectra.shape[0], ir_spectra.shape[1]
    ir = ir_spectra.reshape(rooms, parts, 2, W // 128, 128)
    ir = ir.transpose(0, 1, 3, 2, 4).reshape(rooms, parts, SUB, 128)
    hbm = pl.BlockSpec(memory_space=pltpu.HBM)
    bf16, f32, dma = jnp.bfloat16, jnp.float32, pltpu.SemaphoreType.DMA
    return pl.pallas_call(
        kernel,
        out_shape=jax.ShapeDtypeStruct((ROWS, W), f32),
        in_specs=[hbm] * 6,
        out_specs=pl.BlockSpec(memory_space=pltpu.VMEM),
        scratch_shapes=[
            pltpu.VMEM((W // 2, 2 * W), bf16),
            pltpu.VMEM((2 * W, W // 2), bf16),
            pltpu.VMEM((2, ROOMS, 8, SUB, 128), bf16),
            pltpu.VMEM((NONE + 1, 3, 8, 128), f32),
            pltpu.VMEM((128, 128), f32),
            pltpu.VMEM((PAIRS, 2, ROWS, W), bf16),
            pltpu.VMEM((32 * SUB, 128), f32),
            pltpu.VMEM((SPAN * SUB, 128), f32),
            pltpu.VMEM((2, 8, 128), f32),
            pltpu.VMEM((32 * SUB, 128), f32),
            pltpu.VMEM((8, ROWS, W), bf16),
            pltpu.VMEM((CHIPS, ROWS, W), bf16),
            pltpu.VMEM((8, 128), jnp.int32),
            pltpu.VMEM((8, 128), f32),
            pltpu.SMEM((8, 128), jnp.int32),
            pltpu.SMEM((8, 128), f32),
            pltpu.SMEM((ROOMS,), jnp.int32),
            pltpu.SMEM((ROOMS,), jnp.int32),
            dma((4,)),
            dma((2,)),
            dma,
            dma,
            dma,
            dma((PAIRS, 2)),
            dma((PAIRS, 2)),
            dma((8,)),
            dma((CHIPS,)),
        ],
        compiler_params=pltpu.CompilerParams(
            collective_id=0, has_side_effects=True, vmem_limit_bytes=67_043_328
        ),
    )(samples, ir, clip_lengths, room_ids, forward_part(W), inverse_part(W))


def solution(mesh):
    in_specs = (P(("tile", "ir"), None), P(None, "ir", None, None), P(), P())
    out_specs = P(("tile", "ir"), None)
    return jax.shard_map(
        on_device, mesh=mesh, in_specs=in_specs, out_specs=out_specs, check_vma=False
    )
```

time: 32.7 us -> 30.5 us (0.933)
  the two profiles are of different devices: /device:TPU:1 before, /device:TPU:33 now
where the time goes in v3:
time: 30.5 us; the launch traced here: 30.3 us
  Pallas kernels  29 us (95%)
  local copies, waits for them, and re-layouts  1.38 us (5%)
    pallas_call x1, Pallas kernels, on_device(): pl.pallas_call(kernel, out_shape=jax.ShapeDtypeStruct((ROWS, W), f32), in...  29 us
    unnamed x1, local copies, waits for them, and re-layouts  1.38 us

profile of v3, /device:TPU:33, one launch (start us, length us, event | category | flops | bytes accessed | tf_op | source)
XLA Modules:
  0.0 30.3 jit_solution(2009541142313868107)
XLA Ops:
  0.0 29.0 %shard_map.64 = f32[8,1024]{1,0:T(8,128)} custom-call(bf16[8,1024]{1,0:T(8,128)(2,1)} %samples.1, bf16[16,8,16,128]{3,2,1,0:T(8,128)(2,1)} %bitcast.5, s32[16]{0:T(128)} %lengths.1, s32[16]{0:T(128)} %rooms.1, bf16[512,2048]{1,0:T(8,128)(2,1)} %constant.8.forward, bf16[2048,512]{1,0:T(8,128)(2,1)} %constant.9.inverse), custom_call_target="tpu_custom_call" | custom-call | tf_op jit(solution)/shard_map/pallas_call | solution.py:373
  29.0 1.4 %copy.9 = f32[8,1024]{1,0:T(8,128)} copy(f32[8,1024]{1,0:T(8,128)} %shard_map.64) | data formatting | bytes 65536

commit v4 on v3

v4 whole, which is shorter than its diff:
```python
import jax
import jax.numpy as jnp
import numpy as np
from jax import lax
from jax.experimental import pallas as pl
from jax.experimental.pallas import tpu as pltpu
from jax.sharding import PartitionSpec as P

MESH = pl.DeviceIdType.MESH
W = 1024
ROWS = 8
CHIPS = 8
ROOMS = 16
PARTS = 16
OUT = 64
PAIRS = 5
SPAN = PAIRS * 2 * ROWS
SUB = 2 * W // 128
NONE = ROOMS * PARTS


def forward_part(width):
    length = 2 * width
    sample = np.arange(width // 2)
    bins = np.arange(width)
    phase = sample[:, None] * bins[None, :] % length
    angle = phase * (2.0 * np.pi / length)
    parity = np.where(sample % 2 == 0, 1.0, -1.0)
    sines = np.where(bins[None, :] == 0, parity[:, None], -np.sin(angle))
    table = np.concatenate([np.cos(angle), sines], axis=1)
    return jnp.asarray(table, dtype=jnp.float32).astype(jnp.bfloat16)


def inverse_part(width):
    length = 2 * width
    bins = np.arange(width)
    outputs = width + np.arange(width // 2)
    phase = bins[:, None] * outputs[None, :] % length
    angle = phase * (2.0 * np.pi / length)
    weight = np.where(bins == 0, 1.0, 2.0)[:, None] / length
    parity = np.where(outputs % 2 == 0, 1.0, -1.0)[None, :] / length
    cosines = weight * np.cos(angle)
    sines = np.where(bins[:, None] == 0, parity, -weight * np.sin(angle))
    table = np.concatenate([cosines, sines], axis=0)
    return jnp.asarray(table, dtype=jnp.float32).astype(jnp.bfloat16)


def kernel(
    samples,
    ir,
    lengths,
    rooms,
    forward,
    inverse,
    out,
    fwd_v,
    inv_v,
    ir_v,
    filters,
    unpacked,
    held,
    raw,
    spectra,
    edges_v,
    summed,
    parts_out,
    arrived,
    out_v,
    choice_v,
    first_v,
    choice,
    first,
    lengths_s,
    rooms_s,
    small_sem,
    table_sem,
    ir_send,
    ir_recv,
    ir_own,
    in_send,
    in_recv,
    out_send,
    out_recv,
):
    tile, ir_at = lax.axis_index("tile"), lax.axis_index("ir")
    tiles = lax.axis_size("tile")
    z, c = ir_at // 2, ir_at % 2
    upper = z // 4
    turn = z - 4 * upper
    other = 2 * z + 1 - c
    far_first = (4, 3, 5, 2, 6, 1, 7, 0)

    get_lengths = pltpu.make_async_copy(lengths, lengths_s, small_sem.at[0])
    get_rooms = pltpu.make_async_copy(rooms, rooms_s, small_sem.at[1])
    get_lengths.start()
    get_rooms.start()

    @pl.when(tile == 0)
    def _():
        held[...] = jnp.zeros(held.shape, held.dtype)
        arrived[...] = jnp.zeros(arrived.shape, arrived.dtype)

    barrier = pltpu.get_barrier_semaphore()

    def flag(x):
        return x.astype(jnp.int32)

    def greet(to):
        pl.semaphore_signal(barrier, inc=1, device_id=to, device_id_type=MESH)

    def sum_source(at):
        from_upper = at // 4
        before = from_upper * (1 - upper)
        core = upper + from_upper * (1 - 2 * upper)
        real = ((before == 0) | (tile > 0)) & ((at != z) | (before == 1) | (core != c))
        return (tile - before, 2 * at + core), real

    for away in far_first:
        at = (z + away) % 8
        e = (z + turn + away + 9 - 4 * c) % 8
        before = flag(4 * c + e < turn + 1)
        for k in range(2):
            real = (e < PAIRS) & ((before == 0) | (tile > 0))
            if away == 0:
                real = real & ((before == 1) | (c != k))

            @pl.when(real)
            def _(before=before, at=at, k=k):
                greet((tile - before, 2 * at + k))

        to, real = sum_source(at)

        @pl.when(real)
        def _(to=to):
            greet(to)

    greet((tile, other))

    get_own = pltpu.make_async_copy(ir, ir_v.at[c], ir_own)
    get_own.start()
    get_forward = pltpu.make_async_copy(forward, fwd_v, table_sem.at[0])
    get_forward.start()
    get_inverse = pltpu.make_async_copy(inverse, inv_v, table_sem.at[1])
    get_inverse.start()

    def sample_target(away, d):
        at = (z + away) % 8
        back = at - 4 * (at // 4)
        e = (z + back + 9 - 4 * d) % 8
        ahead = flag(4 * d + e < back + 1)
        there = (e < PAIRS) & ((ahead == 0) | (tile < tiles - 1))
        itself = (away == 0) & (e < PAIRS) & (ahead == 0) & (d == c)
        return at, e, ahead, there, itself

    def sum_target(g, k):
        ahead = upper * c
        at = 4 * (upper + c - 2 * ahead) + g
        there = (ahead == 0) | (tile < tiles - 1)
        itself = (ahead == 0) & (at == z) & (k == c)
        return (tile + ahead, 2 * at + k), there, itself

    awaited = jnp.int32(1)
    for away in range(CHIPS):
        for d in range(2):
            _, _, _, there, itself = sample_target(away, d)
            awaited = awaited + flag(there & jnp.logical_not(itself))
    for g in range(4):
        for k in range(2):
            _, there, itself = sum_target(g, k)
            awaited = awaited + flag(there & jnp.logical_not(itself))
    pl.semaphore_wait(barrier, awaited)

    for away in far_first[::-1]:
        for d in range(2):
            at, e, ahead, there, itself = sample_target(away, d)
            if away == 0:

                @pl.when(itself)
                def _(e=e):
                    pltpu.make_async_copy(samples, held.at[e, c], in_recv.at[e, c]).start()

            @pl.when(there & jnp.logical_not(itself))
            def _(at=at, e=e, ahead=ahead, away=away, d=d):
                pltpu.make_async_remote_copy(
                    src_ref=samples,
                    dst_ref=held.at[e, c],
                    send_sem=in_send.at[away, d],
                    recv_sem=in_recv.at[e, c],
                    device_id=(tile + ahead, 2 * at + d),
                    device_id_type=MESH,
                ).start()

    send_ir = pltpu.make_async_remote_copy(
        src_ref=ir,
        dst_ref=ir_v.at[c],
        send_sem=ir_send,
        recv_sem=ir_recv,
        device_id=(tile, other),
        device_id_type=MESH,
    )
    send_ir.start()

    get_lengths.wait()
    get_rooms.wait()
    place = lax.broadcasted_iota(jnp.int32, (8, 128), 0) * 128 + lax.broadcasted_iota(
        jnp.int32, (8, 128), 1
    )
    base = tile * (2 * OUT) + (upper + c) * OUT
    block = base + place // PARTS
    delay = z * PARTS + place % PARTS
    row_block = base - z * PARTS - PARTS + place
    begin = jnp.zeros((8, 128), jnp.int32)
    room = jnp.zeros((8, 128), jnp.int32)
    joined = jnp.ones((8, 128), jnp.float32)
    start = jnp.int32(0)
    for n in range(ROOMS):
        end = start + lengths_s[n]
        member = (block >= start) & (block < end)
        begin = jnp.where(member, start, begin)
        room = jnp.where(member, rooms_s[n], room)
        joined = jnp.where(row_block == start, 0.0, joined)
        start = end
    chosen = jnp.where(block - delay >= begin, room * PARTS + place % PARTS, NONE)
    choice_v[...] = chosen
    first_v[...] = joined
    put_choice = pltpu.make_async_copy(choice_v, choice, small_sem.at[2])
    put_first = pltpu.make_async_copy(first_v, first, small_sem.at[3])
    put_choice.start()
    put_first.start()

    corner = (lax.broadcasted_iota(jnp.int32, (8, 128), 0) == 0) & (
        lax.broadcasted_iota(jnp.int32, (8, 128), 1) == 0
    )
    filters[NONE] = jnp.zeros((3, 8, 128), jnp.float32)

    def unpack(part):
        def step(n, _):
            for p in range(8):
                unpacked[pl.ds(16 * p, 16), :] = ir_v[part, n, p].astype(jnp.float32)
            for p in range(8):
                hre = unpacked[pl.ds(16 * p, 8, stride=2), :]
                him = unpacked[pl.ds(16 * p + 1, 8, stride=2), :]
                at = n * PARTS + part * 8 + p
                filters[at, 0] = hre
                filters[at, 1] = jnp.where(corner, 0.0, him)
                filters[at, 2] = jnp.where(corner, him, hre)
            return 0

        lax.fori_loop(0, ROOMS, step, 0)

    get_own.wait()
    unpack(c)

    put_choice.wait()
    put_first.wait()
    get_forward.wait()
    get_inverse.wait()
    send_ir.wait_recv()
    unpack(1 - c)

    lane = lax.broadcasted_iota(jnp.int32, (8, 128), 1) % 4
    turn_re = jnp.where(lane == 0, 1.0, jnp.where(lane == 2, -1.0, 0.0))
    turn_im = jnp.where(lane == 1, 1.0, jnp.where(lane == 3, -1.0, 0.0))
    sign = 1.0 - 2.0 * (lane % 2).astype(jnp.float32)

    down = ((z + 4 - 2 * (upper + c)) % 4 + 1) // 2 % 2

    def frame(row, opens, before_re, before_im, own_re, own_im):
        frame_re = opens * before_re + sign * own_re
        frame_im = opens * before_im + sign * own_im
        to = pl.multiple_of(SUB * row, 8)
        spectra[pl.ds(to, 8), :] = frame_re.astype(jnp.bfloat16).astype(jnp.float32)
        spectra[pl.ds(to + 8, 8), :] = frame_im.astype(jnp.bfloat16).astype(jnp.float32)

    def pair(step, _):
        e = step + down * (PAIRS - 1 - 2 * step)

        @pl.when((tile > 0) | (4 * c + e >= turn + 1))
        def _():
            for k in range(2):
                pltpu.make_async_copy(samples, held.at[e, k], in_recv.at[e, k]).wait()

        x = held[e].astype(jnp.float32).reshape(16, W)
        x = jnp.concatenate([x[:, : W // 2], x[:, W // 2 :]], axis=0).astype(jnp.bfloat16)
        for n in range(2 * W // 256):
            g = jnp.dot(x, fwd_v[:, 256 * n : 256 * n + 256], preferred_element_type=jnp.float32)
            raw[pl.ds(2 * n, 32, stride=SUB), :] = g[:, :128]
            raw[pl.ds(2 * n + 1, 32, stride=SUB), :] = g[:, 128:]
        before_re, before_im = None, None
        for r in range(16):
            first_re, first_im = raw[SUB * r : SUB * r + 8, :], raw[SUB * r + 8 : SUB * r + 16, :]
            at = SUB * (16 + r)
            then_re, then_im = raw[at : at + 8, :], raw[at + 8 : at + 16, :]
            own_re = first_re + (turn_re * then_re + turn_im * then_im)
            own_im = first_im + (turn_re * then_im - turn_im * then_re)
            if r == 0:
                edges_v[e, 0, 0] = own_re
                edges_v[e, 0, 1] = own_im
            else:
                frame(16 * e + r, first[0, 16 * e + r], before_re, before_im, own_re, own_im)
            before_re, before_im = own_re, own_im
        edges_v[e, 1, 0] = before_re
        edges_v[e, 1, 1] = before_im

        @pl.when((step == 2) | (step == 4))
        def _():
            h32 = flag(step == 2 + 2 * (1 - down))
            for n in range(2):
                b = 2 * h32 + n
                row = 16 * b + 16
                tail_re, tail_im = edges_v[b, 1, 0], edges_v[b, 1, 1]
                head_re, head_im = edges_v[b + 1, 0, 0], edges_v[b + 1, 0, 1]
                frame(row, first[0, row], tail_re, tail_im, head_re, head_im)

            def eight(b, _):
                res = [jnp.zeros((8, 128), jnp.float32) for _ in range(8)]
                ims = [jnp.zeros((8, 128), jnp.float32) for _ in range(8)]
                for p in range(PARTS):
                    for t in range(8):
                        at = pl.multiple_of(SUB * (32 * h32 + 8 * b + t - p + PARTS), 8)
                        are = spectra[pl.ds(at, 8), :]
                        aim = spectra[pl.ds(at + 8, 8), :]
                        h = choice[4 * h32 + b, 16 * t + p]
                        h0, h1, h2 = filters[h, 0], filters[h, 1], filters[h, 2]
                        res[t] = res[t] + (are * h0 - aim * h1)
                        ims[t] = ims[t] + (are * h1 + aim * h2)
                for t in range(8):
                    to = pl.multiple_of(SUB * (8 * b + t), 8)
                    summed[pl.ds(to, 8), :] = res[t]
                    summed[pl.ds(to + 8, 8), :] = ims[t]
                    summed[pl.ds(32 * SUB + to, 8), :] = turn_re * res[t] - turn_im * ims[t]
                    summed[pl.ds(32 * SUB + to + 8, 8), :] = turn_re * ims[t] + turn_im * res[t]
                return 0

            lax.fori_loop(0, 4, eight, 0)

            y = jnp.concatenate(
                [summed[pl.ds(j, 64, stride=SUB), :].astype(jnp.bfloat16) for j in range(SUB)],
                axis=1,
            )
            for n in range(W // 512):
                v = jnp.dot(
                    y, inv_v[:, 256 * n : 256 * n + 256], preferred_element_type=jnp.float32
                )
                for q in range(8):
                    left = 512 * (q // 4) + 256 * n
                    parts_out[4 * h32 + q % 4, :, left : left + 256] = v[8 * q : 8 * q + 8].astype(
                        jnp.bfloat16
                    )
            for in_half in range(2):
                g = 2 * h32 + in_half
                for k in range(2):
                    to, there, itself = sum_target(g, k)

                    @pl.when(itself)
                    def _(k=k, g=g):
                        pltpu.make_async_copy(
                            parts_out.at[2 * g + k], arrived.at[z], out_recv.at[z]
                        ).start()

                    @pl.when(there & jnp.logical_not(itself))
                    def _(k=k, g=g, to=to):
                        pltpu.make_async_remote_copy(
                            src_ref=parts_out.at[2 * g + k],
                            dst_ref=arrived.at[z],
                            send_sem=out_send.at[2 * g + k],
                            recv_sem=out_recv.at[z],
                            device_id=to,
                            device_id_type=MESH,
                        ).start()

        return 0

    lax.fori_loop(0, PAIRS, pair, 0)

    total = jnp.zeros((ROWS, W), jnp.float32)
    for zs in range(CHIPS):

        @pl.when((tile > 0) | (upper == 1) | (zs < 4))
        def _(zs=zs):
            pltpu.make_async_copy(parts_out.at[0], arrived.at[zs], out_recv.at[zs]).wait()

        total = total + arrived[zs].astype(jnp.float32)
    out_v[...] = total
    put_out = pltpu.make_async_copy(out_v, out, small_sem.at[2])
    put_out.start()

    send_ir.wait_send()
    for away in range(CHIPS):
        for d in range(2):
            _, _, _, there, itself = sample_target(away, d)

            @pl.when(there & jnp.logical_not(itself))
            def _(away=away, d=d):
                pltpu.make_async_copy(samples, held.at[0, 0], in_send.at[away, d]).wait()

    for g in range(4):
        for k in range(2):
            _, there, itself = sum_target(g, k)

            @pl.when(there & jnp.logical_not(itself))
            def _(g=g, k=k):
                pltpu.make_async_copy(
                    parts_out.at[2 * g + k], arrived.at[0], out_send.at[2 * g + k]
                ).wait()

    put_out.wait()


def on_device(samples, ir_spectra, clip_lengths, room_ids):
    rooms, parts = ir_spectra.shape[0], ir_spectra.shape[1]
    ir = ir_spectra.reshape(rooms, parts, 2, W // 128, 128)
    ir = ir.transpose(0, 1, 3, 2, 4).reshape(rooms, parts, SUB, 128)
    hbm = pl.BlockSpec(memory_space=pltpu.HBM)
    bf16, f32, dma = jnp.bfloat16, jnp.float32, pltpu.SemaphoreType.DMA
    return pl.pallas_call(
        kernel,
        out_shape=jax.ShapeDtypeStruct((ROWS, W), f32),
        in_specs=[hbm] * 6,
        out_specs=pl.BlockSpec(memory_space=pltpu.HBM),
        scratch_shapes=[
            pltpu.VMEM((W // 2, 2 * W), bf16),
            pltpu.VMEM((2 * W, W // 2), bf16),
            pltpu.VMEM((2, ROOMS, 8, SUB, 128), bf16),
            pltpu.VMEM((NONE + 1, 3, 8, 128), f32),
            pltpu.VMEM((128, 128), f32),
            pltpu.VMEM((PAIRS, 2, ROWS, W), bf16),
            pltpu.VMEM((32 * SUB, 128), f32),
            pltpu.VMEM((SPAN * SUB, 128), f32),
            pltpu.VMEM((PAIRS, 2, 2, 8, 128), f32),
            pltpu.VMEM((64 * SUB, 128), f32),
            pltpu.VMEM((8, ROWS, W), bf16),
            pltpu.VMEM((CHIPS, ROWS, W), bf16),
            pltpu.VMEM((ROWS, W), f32),
            pltpu.VMEM((8, 128), jnp.int32),
            pltpu.VMEM((8, 128), f32),
            pltpu.SMEM((8, 128), jnp.int32),
            pltpu.SMEM((8, 128), f32),
            pltpu.SMEM((ROOMS,), jnp.int32),
            pltpu.SMEM((ROOMS,), jnp.int32),
            dma((4,)),
            dma((2,)),
            dma,
            dma,
            dma,
            dma((CHIPS, 2)),
            dma((PAIRS, 2)),
            dma((8,)),
            dma((CHIPS,)),
        ],
        compiler_params=pltpu.CompilerParams(
            collective_id=0, has_side_effects=True, vmem_limit_bytes=67_043_328
        ),
    )(samples, ir, clip_lengths, room_ids, forward_part(W), inverse_part(W))


def solution(mesh):
    in_specs = (P(("tile", "ir"), None), P(None, "ir", None, None), P(), P())
    out_specs = P(("tile", "ir"), None)
    return jax.shard_map(
        on_device, mesh=mesh, in_specs=in_specs, out_specs=out_specs, check_vma=False
    )
```

time: 30.5 us -> 30.3 us (level)
  the two profiles are of different devices: /device:TPU:33 before, /device:TPU:57 now
where the time goes in v4:
time: 30.3 us; the launch traced here: 30.1 us
  Pallas kernels  28.7 us (95%)
  local copies, waits for them, and re-layouts  1.38 us (5%)
    pallas_call x1, Pallas kernels, on_device(): pl.pallas_call(kernel, out_shape=jax.ShapeDtypeStruct((ROWS, W), f32), in...  28.7 us
    unnamed x1, local copies, waits for them, and re-layouts  1.38 us

profile of v4, /device:TPU:57, one launch (start us, length us, event | category | flops | bytes accessed | tf_op | source)
XLA Modules:
  0.0 30.1 jit_solution(15045725070610086996)
XLA Ops:
  0.0 28.7 %shard_map.64 = f32[8,1024]{1,0:T(8,128)} custom-call(bf16[8,1024]{1,0:T(8,128)(2,1)} %samples.1, bf16[16,8,16,128]{3,2,1,0:T(8,128)(2,1)} %bitcast.5, s32[16]{0:T(128)} %lengths.1, s32[16]{0:T(128)} %rooms.1, bf16[512,2048]{1,0:T(8,128)(2,1)} %constant.8.forward, bf16[2048,512]{1,0:T(8,128)(2,1)} %constant.9.inverse), custom_call_target="tpu_custom_call" | custom-call | tf_op jit(solution)/shard_map/pallas_call | solution.py:416
  28.8 1.4 %copy.9 = f32[8,1024]{1,0:T(8,128)} copy(f32[8,1024]{1,0:T(8,128)} %shard_map.64) | data formatting | bytes 65536

commit v5 on v4

--- a/solution.py
+++ b/solution.py
@@ -52,20 +52,19 @@
     rooms,
     forward,
     inverse,
-    out,
+    arrived,
     fwd_v,
     inv_v,
     ir_v,
     filters,
     unpacked,
+    mine,
     held,
     raw,
     spectra,
     edges_v,
     summed,
     parts_out,
-    arrived,
-    out_v,
     choice_v,
     first_v,
     choice,
@@ -92,13 +91,18 @@
 
     get_lengths = pltpu.make_async_copy(lengths, lengths_s, small_sem.at[0])
     get_rooms = pltpu.make_async_copy(rooms, rooms_s, small_sem.at[1])
+    get_samples = pltpu.make_async_copy(samples, mine, small_sem.at[3])
+    get_samples.start()
     get_lengths.start()
     get_rooms.start()
 
     @pl.when(tile == 0)
     def _():
         held[...] = jnp.zeros(held.shape, held.dtype)
-        arrived[...] = jnp.zeros(arrived.shape, arrived.dtype)
+        parts_out[...] = jnp.zeros(parts_out.shape, parts_out.dtype)
+        clear = pltpu.make_async_copy(parts_out, arrived, small_sem.at[2])
+        clear.start()
+        clear.wait()
 
     barrier = pltpu.get_barrier_semaphore()
 
@@ -159,30 +163,28 @@
         itself = (ahead == 0) & (at == z) & (k == c)
         return (tile + ahead, 2 * at + k), there, itself
 
-    awaited = jnp.int32(1)
-    for away in range(CHIPS):
-        for d in range(2):
-            _, _, _, there, itself = sample_target(away, d)
-            awaited = awaited + flag(there & jnp.logical_not(itself))
-    for g in range(4):
-        for k in range(2):
-            _, there, itself = sum_target(g, k)
-            awaited = awaited + flag(there & jnp.logical_not(itself))
+    _, _, _, _, own_is_in = sample_target(0, c)
+    _, _, own_is_out = sum_target(z % 4, c)
+    last = flag(tile == tiles - 1)
+    awaited = 1 + 2 * PAIRS + CHIPS - flag(own_is_in) - flag(own_is_out)
+    awaited = awaited - last * (2 * jnp.maximum(z - 3, 0) + 8 * upper * c)
+    get_samples.wait()
     pl.semaphore_wait(barrier, awaited)
 
-    for away in far_first[::-1]:
-        for d in range(2):
+    for window in range(2):
+        for away in far_first[::-1]:
+            d = ((z + away) % 8 // 4 + window) % 2
             at, e, ahead, there, itself = sample_target(away, d)
             if away == 0:
 
                 @pl.when(itself)
                 def _(e=e):
-                    pltpu.make_async_copy(samples, held.at[e, c], in_recv.at[e, c]).start()
+                    pltpu.make_async_copy(mine, held.at[e, c], in_recv.at[e, c]).start()
 
             @pl.when(there & jnp.logical_not(itself))
             def _(at=at, e=e, ahead=ahead, away=away, d=d):
                 pltpu.make_async_remote_copy(
-                    src_ref=samples,
+                    src_ref=mine,
                     dst_ref=held.at[e, c],
                     send_sem=in_send.at[away, d],
                     recv_sem=in_recv.at[e, c],
@@ -264,6 +266,8 @@
     sign = 1.0 - 2.0 * (lane % 2).astype(jnp.float32)
 
     down = ((z + 4 - 2 * (upper + c)) % 4 + 1) // 2 % 2
+    late = down * ((upper + c + 1) % 2)
+    swap = down - late
 
     def frame(row, opens, before_re, before_im, own_re, own_im):
         frame_re = opens * before_re + sign * own_re
@@ -302,9 +306,8 @@
         edges_v[e, 1, 0] = before_re
         edges_v[e, 1, 1] = before_im
 
-        @pl.when((step == 2) | (step == 4))
-        def _():
-            h32 = flag(step == 2 + 2 * (1 - down))
+        def half_sums(m, _):
+            h32 = m + swap * (1 - 2 * m)
             for n in range(2):
                 b = 2 * h32 + n
                 row = 16 * b + 16
@@ -369,21 +372,14 @@
                             device_id_type=MESH,
                         ).start()
 
+            return 0
+
+        at_third, at_last = flag(step == 2), flag(step == 4)
+        begun = at_last * (1 - late)
+        lax.fori_loop(begun, at_third * (1 - late) + 2 * at_last, half_sums, 0)
         return 0
 
     lax.fori_loop(0, PAIRS, pair, 0)
-
-    total = jnp.zeros((ROWS, W), jnp.float32)
-    for zs in range(CHIPS):
-
-        @pl.when((tile > 0) | (upper == 1) | (zs < 4))
-        def _(zs=zs):
-            pltpu.make_async_copy(parts_out.at[0], arrived.at[zs], out_recv.at[zs]).wait()
-
-        total = total + arrived[zs].astype(jnp.float32)
-    out_v[...] = total
-    put_out = pltpu.make_async_copy(out_v, out, small_sem.at[2])
-    put_out.start()
 
     send_ir.wait_send()
     for away in range(CHIPS):
@@ -404,7 +400,11 @@
                     parts_out.at[2 * g + k], arrived.at[0], out_send.at[2 * g + k]
                 ).wait()
 
-    put_out.wait()
+    for zs in range(CHIPS):
+
+        @pl.when((tile > 0) | (upper == 1) | (zs < 4))
+        def _(zs=zs):
+            pltpu.make_async_copy(parts_out.at[0], arrived.at[zs], out_recv.at[zs]).wait()
 
 
 def on_device(samples, ir_spectra, clip_lengths, room_ids):
@@ -413,9 +413,9 @@
     ir = ir.transpose(0, 1, 3, 2, 4).reshape(rooms, parts, SUB, 128)
     hbm = pl.BlockSpec(memory_space=pltpu.HBM)
     bf16, f32, dma = jnp.bfloat16, jnp.float32, pltpu.SemaphoreType.DMA
-    return pl.pallas_call(
+    arrived = pl.pallas_call(
         kernel,
-        out_shape=jax.ShapeDtypeStruct((ROWS, W), f32),
+        out_shape=jax.ShapeDtypeStruct((CHIPS, ROWS, W), bf16),
         in_specs=[hbm] * 6,
         out_specs=pl.BlockSpec(memory_space=pltpu.HBM),
         scratch_shapes=[
@@ -424,14 +424,13 @@
             pltpu.VMEM((2, ROOMS, 8, SUB, 128), bf16),
             pltpu.VMEM((NONE + 1, 3, 8, 128), f32),
             pltpu.VMEM((128, 128), f32),
+            pltpu.VMEM((ROWS, W), bf16),
             pltpu.VMEM((PAIRS, 2, ROWS, W), bf16),
             pltpu.VMEM((32 * SUB, 128), f32),
             pltpu.VMEM((SPAN * SUB, 128), f32),
             pltpu.VMEM((PAIRS, 2, 2, 8, 128), f32),
             pltpu.VMEM((64 * SUB, 128), f32),
             pltpu.VMEM((8, ROWS, W), bf16),
-            pltpu.VMEM((CHIPS, ROWS, W), bf16),
-            pltpu.VMEM((ROWS, W), f32),
             pltpu.VMEM((8, 128), jnp.int32),
             pltpu.VMEM((8, 128), f32),
             pltpu.SMEM((8, 128), jnp.int32),
@@ -452,6 +451,7 @@
             collective_id=0, has_side_effects=True, vmem_limit_bytes=67_043_328
         ),
     )(samples, ir, clip_lengths, room_ids, forward_part(W), inverse_part(W))
+    return jnp.sum(arrived.astype(f32), axis=0)
 
 
 def solution(mesh):

time: 30.3 us -> 28.2 us (0.931)
  Pallas kernels: 28.7 us -> 26.5 us
  other arithmetic: 0 us -> 1.54 us
  local copies, waits for them, and re-layouts: 1.38 us -> 0 us
    pallas_call x1, Pallas kernels: 28.7 us -> 26.5 us  [on_device(): pl.pallas_call(kernel, out_shape=jax.ShapeDtypeStruct((CHIPS, ROWS, W), b...]
    reduce_sum x0 -> x1, other arithmetic: none -> 1.54 us  [on_device(): return jnp.sum(arrived.astype(f32), axis=0)]
    unnamed x1 -> x0, local copies, waits for them, and re-layouts: 1.38 us -> none
where the time goes in v5:
time: 28.2 us; the launch traced here: 28.1 us
  Pallas kernels  26.5 us (94%)
  other arithmetic  1.54 us (5%)
    pallas_call x1, Pallas kernels, on_device(): pl.pallas_call(kernel, out_shape=jax.ShapeDtypeStruct((CHIPS, ROWS, W), b...  26.5 us
    reduce_sum x1, other arithmetic, on_device(): return jnp.sum(arrived.astype(f32), axis=0)  1.54 us

profile of v5, /device:TPU:57, one launch (start us, length us, event | category | flops | bytes accessed | tf_op | source)
XLA Modules:
  0.0 28.1 jit_solution(5120899092393883479)
XLA Ops:
  0.0 26.5 %shard_map.64 = bf16[8,8,1024]{2,1,0:T(8,128)(2,1)} custom-call(bf16[8,1024]{1,0:T(8,128)(2,1)} %samples.1, bf16[16,8,16,128]{3,2,1,0:T(8,128)(2,1)} %bitcast.5, s32[16]{0:T(128)} %lengths.1, s32[16]{0:T(128)} %rooms.1, bf16[512,2048]{1,0:T(8,128)(2,1)} %constant.10.forward, bf16[2048,512]{1,0:T(8,128)(2,1)} %constant.11.inverse), custom_call_target="tpu_custom_call" | custom-call | tf_op jit(solution)/shard_map/pallas_call | solution.py:416
  26.5 1.5 %convert_reduce_fusion = f32[8,1024]{1,0:T(8,128)} fusion(bf16[8,8,1024]{2,1,0:T(8,128)(2,1)} %shard_map.64), kind=kLoop, calls=%fused_computation | loop fusion | flops 122880 | bytes 163840 | tf_op jit(solution)/shard_map/reduce_sum | solution.py:454

commit v6 on v5

--- a/solution.py
+++ b/solution.py
@@ -52,7 +52,7 @@
     rooms,
     forward,
     inverse,
-    arrived,
+    out,
     fwd_v,
     inv_v,
     ir_v,
@@ -65,6 +65,7 @@
     edges_v,
     summed,
     parts_out,
+    arrived,
     choice_v,
     first_v,
     choice,
@@ -99,10 +100,7 @@
     @pl.when(tile == 0)
     def _():
         held[...] = jnp.zeros(held.shape, held.dtype)
-        parts_out[...] = jnp.zeros(parts_out.shape, parts_out.dtype)
-        clear = pltpu.make_async_copy(parts_out, arrived, small_sem.at[2])
-        clear.start()
-        clear.wait()
+        arrived[...] = jnp.zeros(arrived.shape, arrived.dtype)
 
     barrier = pltpu.get_barrier_semaphore()
 
@@ -266,6 +264,7 @@
     sign = 1.0 - 2.0 * (lane % 2).astype(jnp.float32)
 
     down = ((z + 4 - 2 * (upper + c)) % 4 + 1) // 2 % 2
+    down = jnp.maximum(down, flag((z == 0) & (c == 0)))
     late = down * ((upper + c + 1) % 2)
     swap = down - late
 
@@ -400,11 +399,15 @@
                     parts_out.at[2 * g + k], arrived.at[0], out_send.at[2 * g + k]
                 ).wait()
 
+    total = jnp.zeros((ROWS, W), jnp.float32)
     for zs in range(CHIPS):
 
         @pl.when((tile > 0) | (upper == 1) | (zs < 4))
         def _(zs=zs):
             pltpu.make_async_copy(parts_out.at[0], arrived.at[zs], out_recv.at[zs]).wait()
+
+        total = total + arrived[zs].astype(jnp.float32)
+    out[...] = total
 
 
 def on_device(samples, ir_spectra, clip_lengths, room_ids):
@@ -413,11 +416,11 @@
     ir = ir.transpose(0, 1, 3, 2, 4).reshape(rooms, parts, SUB, 128)
     hbm = pl.BlockSpec(memory_space=pltpu.HBM)
     bf16, f32, dma = jnp.bfloat16, jnp.float32, pltpu.SemaphoreType.DMA
-    arrived = pl.pallas_call(
+    return pl.pallas_call(
         kernel,
-        out_shape=jax.ShapeDtypeStruct((CHIPS, ROWS, W), bf16),
+        out_shape=jax.ShapeDtypeStruct((ROWS, W), f32),
         in_specs=[hbm] * 6,
-        out_specs=pl.BlockSpec(memory_space=pltpu.HBM),
+        out_specs=pl.BlockSpec(memory_space=pltpu.VMEM),
         scratch_shapes=[
             pltpu.VMEM((W // 2, 2 * W), bf16),
             pltpu.VMEM((2 * W, W // 2), bf16),
@@ -431,6 +434,7 @@
             pltpu.VMEM((PAIRS, 2, 2, 8, 128), f32),
             pltpu.VMEM((64 * SUB, 128), f32),
             pltpu.VMEM((8, ROWS, W), bf16),
+            pltpu.VMEM((CHIPS, ROWS, W), bf16),
             pltpu.VMEM((8, 128), jnp.int32),
             pltpu.VMEM((8, 128), f32),
             pltpu.SMEM((8, 128), jnp.int32),
@@ -448,10 +452,14 @@
             dma((CHIPS,)),
         ],
         compiler_params=pltpu.CompilerParams(
-            collective_id=0, has_side_effects=True, vmem_limit_bytes=67_043_328
+            collective_id=0, has_side_effects=True, vmem_limit_bytes=48 * 1024 * 1024
         ),
-    )(samples, ir, clip_lengths, room_ids, forward_part(W), inverse_part(W))
-    return jnp.sum(arrived.astype(f32), axis=0)
+    )(
+        *[
+            pltpu.with_memory_space_constraint(x, pltpu.HBM)
+            for x in (samples, ir, clip_lengths, room_ids, forward_part(W), inverse_part(W))
+        ]
+    )
 
 
 def solution(mesh):

time: 28.2 us -> 27.2 us (0.965)
  other arithmetic: 1.54 us -> 0 us
  local copies, waits for them, and re-layouts: 0 us -> 0.62 us
    reduce_sum x1 -> x0, other arithmetic: 1.54 us -> none  [on_device(): return jnp.sum(arrived.astype(f32), axis=0)]
    unnamed x0 -> x1, local copies, waits for them, and re-layouts: none -> 0.62 us
where the time goes in v6:
time: 27.2 us; the launch traced here: 27 us
  Pallas kernels  26.4 us (97%)
  local copies, waits for them, and re-layouts  0.62 us (2%)
    pallas_call x1, Pallas kernels, on_device(): pl.pallas_call(kernel, out_shape=jax.ShapeDtypeStruct((ROWS, W), f32), in...  26.4 us
    unnamed x1, local copies, waits for them, and re-layouts  0.62 us

profile of v6, /device:TPU:57, one launch (start us, length us, event | category | flops | bytes accessed | tf_op | source)
XLA Modules:
  0.0 27.0 jit_solution(7212436778147233641)
XLA Ops:
  0.0 26.4 %shard_map.64 = f32[8,1024]{1,0:T(8,128)S(1)} custom-call(bf16[8,1024]{1,0:T(8,128)(2,1)} %samples.1, bf16[16,8,16,128]{3,2,1,0:T(8,128)(2,1)} %bitcast.5, s32[16]{0:T(128)} %lengths.1, s32[16]{0:T(128)} %rooms.1, bf16[512,2048]{1,0:T(8,128)(2,1)} %constant.8.forward, bf16[2048,512]{1,0:T(8,128)(2,1)} %constant.9.inverse), custom_call_target="tpu_custom_call" | custom-call | tf_op jit(solution)/shard_map/pallas_call | solution.py:419
  26.4 0.6 %copy.9 = f32[8,1024]{1,0:T(8,128)} copy(f32[8,1024]{1,0:T(8,128)S(1)} %shard_map.64) | data formatting | bytes 65536

commit v7 on v6

--- a/solution.py
+++ b/solution.py
@@ -93,9 +93,6 @@
     get_lengths = pltpu.make_async_copy(lengths, lengths_s, small_sem.at[0])
     get_rooms = pltpu.make_async_copy(rooms, rooms_s, small_sem.at[1])
     get_samples = pltpu.make_async_copy(samples, mine, small_sem.at[3])
-    get_samples.start()
-    get_lengths.start()
-    get_rooms.start()
 
     @pl.when(tile == 0)
     def _():
@@ -137,6 +134,9 @@
             greet(to)
 
     greet((tile, other))
+    get_samples.start()
+    get_lengths.start()
+    get_rooms.start()
 
     get_own = pltpu.make_async_copy(ir, ir_v.at[c], ir_own)
     get_own.start()
@@ -170,7 +170,7 @@
     pl.semaphore_wait(barrier, awaited)
 
     for window in range(2):
-        for away in far_first[::-1]:
+        for away in (1, 2, 3, 4, 7, 6, 5, 0):
             d = ((z + away) % 8 // 4 + window) % 2
             at, e, ahead, there, itself = sample_target(away, d)
             if away == 0:

time: 27.2 us -> 27.1 us (level); the launches traced: 27 us -> 26.5 us
  Pallas kernels: 26.4 us -> 25.9 us
    pallas_call x1, Pallas kernels: 26.4 us -> 25.9 us  [on_device(): pl.pallas_call(kernel, out_shape=jax.ShapeDtypeStruct((ROWS, W), f32), in...]
where the time goes in v7:
time: 27.1 us; the launch traced here: 26.5 us
  Pallas kernels  25.9 us (96%)
  local copies, waits for them, and re-layouts  0.62 us (2%)
    pallas_call x1, Pallas kernels, on_device(): pl.pallas_call(kernel, out_shape=jax.ShapeDtypeStruct((ROWS, W), f32), in...  25.9 us
    unnamed x1, local copies, waits for them, and re-layouts  0.62 us

profile of v7, /device:TPU:57, one launch (start us, length us, event | category | flops | bytes accessed | tf_op | source)
XLA Modules:
  0.0 26.5 jit_solution(9984544844094042633)
XLA Ops:
  0.0 25.9 %shard_map.64 = f32[8,1024]{1,0:T(8,128)S(1)} custom-call(bf16[8,1024]{1,0:T(8,128)(2,1)} %samples.1, bf16[16,8,16,128]{3,2,1,0:T(8,128)(2,1)} %bitcast.5, s32[16]{0:T(128)} %lengths.1, s32[16]{0:T(128)} %rooms.1, bf16[512,2048]{1,0:T(8,128)(2,1)} %constant.8.forward, bf16[2048,512]{1,0:T(8,128)(2,1)} %constant.9.inverse), custom_call_target="tpu_custom_call" | custom-call | tf_op jit(solution)/shard_map/pallas_call | solution.py:419
  25.9 0.6 %copy.9 = f32[8,1024]{1,0:T(8,128)} copy(f32[8,1024]{1,0:T(8,128)S(1)} %shard_map.64) | data formatting | bytes 65536

commit v8 on v7

--- a/solution.py
+++ b/solution.py
@@ -169,7 +169,17 @@
     get_samples.wait()
     pl.semaphore_wait(barrier, awaited)
 
+    send_ir = pltpu.make_async_remote_copy(
+        src_ref=ir,
+        dst_ref=ir_v.at[c],
+        send_sem=ir_send,
+        recv_sem=ir_recv,
+        device_id=(tile, other),
+        device_id_type=MESH,
+    )
     for window in range(2):
+        if window == 1:
+            send_ir.start()
         for away in (1, 2, 3, 4, 7, 6, 5, 0):
             d = ((z + away) % 8 // 4 + window) % 2
             at, e, ahead, there, itself = sample_target(away, d)
@@ -190,15 +200,6 @@
                     device_id_type=MESH,
                 ).start()
 
-    send_ir = pltpu.make_async_remote_copy(
-        src_ref=ir,
-        dst_ref=ir_v.at[c],
-        send_sem=ir_send,
-        recv_sem=ir_recv,
-        device_id=(tile, other),
-        device_id_type=MESH,
-    )
-    send_ir.start()
 
     get_lengths.wait()
     get_rooms.wait()

time: 27.1 us -> 27.1 us (level)
  no operation moved by 1% of the time
where the time goes in v8:
time: 27.1 us; the launch traced here: 26.6 us
  Pallas kernels  26 us (96%)
  local copies, waits for them, and re-layouts  0.62 us (2%)
    pallas_call x1, Pallas kernels, on_device(): pl.pallas_call(kernel, out_shape=jax.ShapeDtypeStruct((ROWS, W), f32), in...  26 us
    unnamed x1, local copies, waits for them, and re-layouts  0.62 us

profile of v8, /device:TPU:57, one launch (start us, length us, event | category | flops | bytes accessed | tf_op | source)
XLA Modules:
  0.0 26.6 jit_solution(15253426576264824262)
XLA Ops:
  0.0 26.0 %shard_map.64 = f32[8,1024]{1,0:T(8,128)S(1)} custom-call(bf16[8,1024]{1,0:T(8,128)(2,1)} %samples.1, bf16[16,8,16,128]{3,2,1,0:T(8,128)(2,1)} %bitcast.5, s32[16]{0:T(128)} %lengths.1, s32[16]{0:T(128)} %rooms.1, bf16[512,2048]{1,0:T(8,128)(2,1)} %constant.8.forward, bf16[2048,512]{1,0:T(8,128)(2,1)} %constant.9.inverse), custom_call_target="tpu_custom_call" | custom-call | tf_op jit(solution)/shard_map/pallas_call | solution.py:420
  26.0 0.6 %copy.9 = f32[8,1024]{1,0:T(8,128)} copy(f32[8,1024]{1,0:T(8,128)S(1)} %shard_map.64) | data formatting | bytes 65536
